TPU v7x, 32 devices: a whole 2x2x4 slice. The times are simulated.
32 devices in a mesh: dp: 8 (over z, core), space: 4 (over y, x).
Axes of the slice: x: 2, y: 2, z: 4, core: 2. Of those that a mesh axis runs over, the one named last changes fastest.
Arguments:
- inputs: bfloat16 [8, 24, 32, 32, 256], P('dp', 'space'), may hold values from -6 to 6
- kernels: bfloat16 [2, 3, 3, 256, 256], P(None, None, None, 'dp'), may hold values from -0.125 to 0.125
- cotangent: bfloat16 [8, 24, 32, 32, 256], P('dp', 'space'), may hold values from -0.01171875 to 0.01171875
- adjacency: int32 [24, 4, 3], P('space'), may hold values from 0 to 23, as said below
Outputs:
- final_state: bfloat16 [8, 24, 32, 32, 256], P('dp', 'space')
- kernel_grads: float32 [2, 3, 3, 256, 256], P(None, None, None, 'dp')
Inputs may be any that keep to these rules, and one draw needn't show every extreme that they name: Entry [t, e] = (n, f, r): edge e of tile t meets edge f of tile n, and r = 1 where the two edges are read in opposite directions along the shared line. The relation is symmetric: adjacency[n, f] = (t, e, r). The tiles form 2 x 2 blocks on the six faces of a cube, numbered in an order drawn from the seed.
All inputs are finite; a program needn't handle non-finite values.
Results may differ from a plain program's by a relative error of at most 0.005.
Values may be sent and summed in bfloat16 or wider, within the bound.
A program may use at most 192 MiB of HBM per device.

v0:
```python
import jax
import jax.numpy as jnp
from jax import lax
from jax.sharding import PartitionSpec as P

LAYERS = 2


def edge_strips(tile_field):
    return jnp.stack(
        [
            tile_field[:, :, 0],
            tile_field[:, :, -1],
            tile_field[:, :, :, 0],
            tile_field[:, :, :, -1],
        ],
        axis=2,
    )


def orient(strips, adjacency):
    selected = strips[:, adjacency[:, :, 0], adjacency[:, :, 1]]
    flipped = (adjacency[:, :, 2] == 1)[None, :, :, None, None]
    return jnp.where(flipped, selected[:, :, :, ::-1], selected)


def neighbor_rims(tile_field, adjacency):
    gathered = lax.all_gather(edge_strips(tile_field), "space", axis=1, tiled=True)
    return orient(gathered, adjacency)


def returned_rims(rim_values, adjacency):
    gathered = lax.all_gather(rim_values, "space", axis=1, tiled=True)
    return orient(gathered, adjacency)


def with_rim(tile_field, rim_rows):
    middle = jnp.concatenate(
        [rim_rows[:, :, 2][:, :, :, None], tile_field, rim_rows[:, :, 3][:, :, :, None]], axis=3
    )
    corner = jnp.zeros(tile_field.shape[:2] + (1, tile_field.shape[4]), tile_field.dtype)
    top_row = jnp.concatenate([corner, rim_rows[:, :, 0], corner], axis=2)[:, :, None]
    bottom_row = jnp.concatenate([corner, rim_rows[:, :, 1], corner], axis=2)[:, :, None]
    return jnp.concatenate([top_row, middle, bottom_row], axis=2)


def convolve(padded, kernel):
    extent = padded.shape[2] - 2
    channels = padded.shape[-1]
    summed = jnp.zeros(padded.shape[:2] + (extent, extent, kernel.shape[-1]), jnp.float32)
    for row_off in range(3):
        for col_off in range(3):
            patches = padded[:, :, row_off : row_off + extent, col_off : col_off + extent].reshape(
                -1, channels
            )
            summed = summed + jnp.dot(
                patches, kernel[row_off, col_off], preferred_element_type=jnp.float32
            ).reshape(summed.shape)
    return summed


def weight_grad(padded, flat_grad):
    extent = padded.shape[2] - 2
    channels = padded.shape[-1]
    rows_out = []
    for row_off in range(3):
        row_list = []
        for col_off in range(3):
            patches = padded[:, :, row_off : row_off + extent, col_off : col_off + extent].reshape(
                -1, channels
            )
            row_list.append(
                lax.dot_general(
                    patches, flat_grad, (((0,), (0,)), ((), ())), preferred_element_type=jnp.float32
                )
            )
        rows_out.append(jnp.stack(row_list))
    return jnp.stack(rows_out)


def input_grad(flat_grad, kernel, padded_shape):
    extent = padded_shape[2] - 2
    full = extent + 2
    channels = padded_shape[4]
    grid_grad = flat_grad.reshape(padded_shape[:2] + (extent, extent, flat_grad.shape[-1]))
    widened = jnp.pad(grid_grad, ((0, 0), (0, 0), (2, 2), (2, 2), (0, 0)))
    pad_grad = jnp.zeros(padded_shape, jnp.float32)
    for row_off in range(3):
        for col_off in range(3):
            window = widened[
                :, :, 2 - row_off : 2 - row_off + full, 2 - col_off : 2 - col_off + full
            ].reshape(-1, flat_grad.shape[-1])
            contrib = lax.dot_general(
                window,
                kernel[row_off, col_off],
                (((1,), (1,)), ((), ())),
                preferred_element_type=jnp.float32,
            )
            pad_grad = pad_grad + contrib.reshape(padded_shape[:4] + (channels,))
    return pad_grad


def rim_strips(pad_grad):
    return jnp.stack(
        [
            pad_grad[:, :, 0, 1:-1],
            pad_grad[:, :, -1, 1:-1],
            pad_grad[:, :, 1:-1, 0],
            pad_grad[:, :, 1:-1, -1],
        ],
        axis=2,
    )


def add_rim(interior, returned):
    interior = jnp.concatenate(
        [
            interior[:, :, :1] + returned[:, :, 0][:, :, None],
            interior[:, :, 1:-1],
            interior[:, :, -1:] + returned[:, :, 1][:, :, None],
        ],
        axis=2,
    )
    interior = jnp.concatenate(
        [
            interior[:, :, :, :1] + returned[:, :, 2][:, :, :, None],
            interior[:, :, :, 1:-1],
            interior[:, :, :, -1:] + returned[:, :, 3][:, :, :, None],
        ],
        axis=3,
    )
    return interior


def reduce_grad(partial_value):
    space_total = lax.psum(partial_value, "space")
    return lax.psum_scatter(space_total, "dp", scatter_dimension=2, tiled=True)


def per_device(inputs, kernels, cotangent, adjacency):
    weights = lax.all_gather(kernels, "dp", axis=3, tiled=True)
    current = inputs
    stored = []
    for layer_num in range(LAYERS):
        padded = with_rim(current, neighbor_rims(current, adjacency))
        preact = convolve(padded, weights[layer_num])
        current = (current.astype(jnp.float32) + jax.nn.silu(preact)).astype(jnp.bfloat16)
        stored.append((padded, preact))
    upstream = cotangent.astype(jnp.float32)
    kernel_grads = [None] * LAYERS
    for layer_num in range(LAYERS - 1, -1, -1):
        padded, preact = stored[layer_num]
        logistic = jax.nn.sigmoid(preact)
        pre_grad = (upstream * logistic * (1.0 + preact * (1.0 - logistic))).astype(jnp.bfloat16)
        flat_grad = pre_grad.reshape(-1, pre_grad.shape[-1])
        kernel_grads[layer_num] = reduce_grad(weight_grad(padded, flat_grad))
        if layer_num > 0:
            pad_grad = input_grad(flat_grad, weights[layer_num], padded.shape)
            rim_values = rim_strips(pad_grad).astype(jnp.bfloat16)
            returned = returned_rims(rim_values, adjacency).astype(jnp.float32)
            upstream = add_rim(upstream + pad_grad[:, :, 1:-1, 1:-1], returned)
    return (current, jnp.stack(kernel_grads))


def solution(mesh):
    in_specs = (
        P("dp", "space", None, None, None),
        P(None, None, None, "dp", None),
        P("dp", "space", None, None, None),
        P("space", None, None),
    )
    out_specs = (P("dp", "space", None, None, None), P(None, None, None, "dp", None))
    return jax.shard_map(
        per_device, mesh=mesh, in_specs=in_specs, out_specs=out_specs, check_vma=False
    )
```

profile of v0, /device:TPU:0, one launch (start us, length us, event | category | flops | bytes accessed | tf_op | source)
XLA Modules:
  0.0 505.8 jit_solution(17748328288666397905)
XLA Ops:
  12.9 32.7 %all-gather.5.cloned.1.call-done = bf16[1,24,4,32,256]{4,3,1,2,0:T(8,128)(2,1)} async-done(((bf16[1,6,4,32,256]{4,3,1,2,0:T(8,128)(2,1)}), bf16[1,24,4,32,256]{4,3,1,2,0:T(8,128)(2,1)}) %all-gather.5.cloned.1.call-update) | async-done | bytes 1572880 | tf_op jit(solution)/shard_map/all_gather | solution.py:28
  51.8 5.4 %fusion.38 = (bf16[6,32,32,256]{3,2,1,0:T(8,128)(2,1)}, bf16[6,32,32,256]{3,2,1,0:T(8,128)(2,1)}) fusion(bf16[1,6,32,32,256]{4,3,2,1,0:T(8,128)(2,1)S(1)} %copy-done.4, bf16[1,6,32,1,256]{4,3,2,1,0:T(2,128)(2,1)S(1)} %copy.109, bf16[1,6,32,1,256]{4,3,2,1,0:T(2,128)(2,1)S(1)} %copy.110), kind=kLoop, calls=%fused_computation.68 | loop fusion | flops 12582912 | bytes 9633792 | tf_op jit(solution)/shard_map/dot_general | solution.py:56
  57.2 4.9 maximum_maximum_fusion.1
  65.4 10.6 %slice_bitcast_fusion.9 = (bf16[6,32,32,256]{3,2,1,0:T(8,128)(2,1)}, bf16[6,32,32,256]{3,2,1,0:T(8,128)(2,1)}, bf16[6,32,32,256]{3,2,1,0:T(8,128)(2,1)}, bf16[6,...) fusion(bf16[1,6,33,34,256]{4,3,2,1,0:T(8,128)(2,1)S(1)} %get-tuple-element.31, ...), kind=kLoop, calls=%fused_computation.64 | loop fusion | bytes 37748736 | tf_op jit(solution)/shard_map/dot_general | solution.py:56
  81.7 6.2 %fusion.60 = f32[6,32,32,256]{3,1,0,2:T(8,128)} fusion(bf16[6,32,32,256]{3,2,1,0:T(8,128)(2,1)S(1)} %copy-done.18, bf16[3,3,256,256]{3,2,1,0:T(8,128)(2,1)S(1)} %get-tuple-element.46), kind=kOutput, calls=%fused_computation.93 | convolution fusion | flops 805306368 | bytes 9568256 | tf_op jit(solution)/shard_map/dot_general | solution.py:56
  88.0 6.2 %fusion.62 = f32[6,32,32,256]{3,1,0,2:T(8,128)} fusion(bf16[6,32,32,256]{3,2,1,0:T(8,128)(2,1)S(1)} %copy-done.17, bf16[3,3,256,256]{3,2,1,0:T(8,128)(2,1)S(1)} %get-tuple-element.46), kind=kOutput, calls=%fused_computation.95 | convolution fusion | flops 805306368 | bytes 9568256 | tf_op jit(solution)/shard_map/dot_general | solution.py:56
  94.2 6.3 %fusion.64 = f32[6,32,32,256]{3,1,0,2:T(8,128)} fusion(bf16[6,32,32,256]{3,2,1,0:T(8,128)(2,1)S(1)} %copy-done.16, bf16[3,3,256,256]{3,2,1,0:T(8,128)(2,1)S(1)} %get-tuple-element.46), kind=kOutput, calls=%fused_computation.97 | convolution fusion | flops 805306368 | bytes 9568256 | tf_op jit(solution)/shard_map/dot_general | solution.py:56
  100.5 6.3 %fusion.66 = f32[6,32,32,256]{3,1,0,2:T(8,128)} fusion(bf16[6,32,32,256]{3,2,1,0:T(8,128)(2,1)S(1)} %copy-done.21, bf16[3,3,256,256]{3,2,1,0:T(8,128)(2,1)S(1)} %get-tuple-element.46), kind=kOutput, calls=%fused_computation.99 | convolution fusion | flops 805306368 | bytes 9568256 | tf_op jit(solution)/shard_map/dot_general | solution.py:56
  106.8 6.3 %fusion.68 = f32[6,32,32,256]{3,1,0,2:T(8,128)} fusion(bf16[6,32,32,256]{3,2,1,0:T(8,128)(2,1)S(1)} %bitcast.431, bf16[3,3,256,256]{3,2,1,0:T(8,128)(2,1)S(1)} %get-tuple-element.46), kind=kOutput, calls=%fused_computation.101 | convolution fusion | flops 805306368 | bytes 9568256 | tf_op jit(solution)/shard_map/dot_general | solution.py:56
  113.1 6.2 %fusion.70 = f32[6,32,32,256]{3,1,0,2:T(8,128)} fusion(bf16[6,32,32,256]{3,2,1,0:T(8,128)(2,1)S(1)} %copy-done.19, bf16[3,3,256,256]{3,2,1,0:T(8,128)(2,1)S(1)} %get-tuple-element.46), kind=kOutput, calls=%fused_computation.103 | convolution fusion | flops 805306368 | bytes 9568256 | tf_op jit(solution)/shard_map/dot_general | solution.py:56
  119.3 6.7 %fusion.72 = f32[6,32,32,256]{3,1,0,2:T(8,128)} fusion(bf16[6,32,32,256]{3,2,1,0:T(8,128)(2,1)S(1)} %copy-done.15, bf16[3,3,256,256]{3,2,1,0:T(8,128)(2,1)S(1)} %get-tuple-element.46), kind=kOutput, calls=%fused_computation.105 | convolution fusion | flops 805306368 | bytes 9568256 | tf_op jit(solution)/shard_map/dot_general | solution.py:56
  126.0 6.2 %fusion.74 = f32[6,32,32,256]{3,1,0,2:T(8,128)} fusion(bf16[6,32,32,256]{3,2,1,0:T(8,128)(2,1)S(1)} %copy-done.14, bf16[3,3,256,256]{3,2,1,0:T(8,128)(2,1)S(1)} %get-tuple-element.46), kind=kOutput, calls=%fused_computation.107 | convolution fusion | flops 805306368 | bytes 9568256 | tf_op jit(solution)/shard_map/dot_general | solution.py:56
  132.2 22.0 %fusion.5 = (bf16[1,6,32,32,256]{4,2,1,3,0:T(8,128)(2,1)S(1)}, f32[6,32,32,256]{3,1,0,2:T(8,128)}) fusion(bf16[1,6,32,32,256]{4,3,2,1,0:T(8,128)(2,1)S(1)} %copy-done.5, f32[6,32,32,256]{3,1,0,2:T(8,128)} %fusion.60, f32[6,32,32,256]{3,1,0,2:T(8,128)} %fusion.62, f32[6,32,32,256]{3,1,0,2:T(8,128)} %fusion.64, f32[6,32,32,256]{3,1,0,2:T(8,128)} %fusion.66, ...), kind=kOutput, calls=%fused_computation.15 | convolution fusion | flops 828899328 | bytes 66191360 | tf_op jit(solution)/shard_map/dot_general | solution.py:56
  155.8 4.5 fusion.141
  160.3 25.7 %all-gather.9.cloned.1.call-done = bf16[1,24,4,32,256]{4,3,1,2,0:T(8,128)(2,1)} async-done(((bf16[1,6,4,32,256]{4,3,1,2,0:T(8,128)(2,1)}), bf16[1,24,4,32,256]{4,3,1,2,0:T(8,128)(2,1)}) %all-gather.9.cloned.1.call-update) | async-done | bytes 1572880 | tf_op jit(solution)/shard_map/all_gather | solution.py:28
  214.8 7.1 %slice_bitcast_fusion.3 = (bf16[6,32,32,256]{3,1,0,2:T(8,128)(2,1)}, bf16[6,32,32,256]{3,1,0,2:T(8,128)(2,1)}, bf16[6,32,32,256]{3,1,0,2:T(8,128)(2,1)}) fusion(bf16[1,6,33,34,256]{4,2,1,3,0:T(8,128)(2,1)S(1)} %get-tuple-element.33), kind=kLoop, calls=%fused_computation.54 | loop fusion | bytes 18874368 | tf_op jit(solution)/shard_map/dot_general | solution.py:56
  229.2 21.6 %fusion.1 = (bf16[1,6,32,32,256]{4,2,1,3,0:T(8,128)(2,1)S(1)}, bf16[1,6,32,32,256]{4,2,1,3,0:T(8,128)(2,1)}) fusion(bf16[1,6,32,32,256]{4,3,2,1,0:T(8,128)(2,1)} %param.6, bf16[1,6,32,32,256]{4,2,1,3,0:T(8,128)(2,1)} %copy-done.2, bf16[3,3,256,256]{3,2,1,0:T(8,128)(2,1)} %get-tuple-element.47, bf16[1,6,33,34,256]{4,2,1,3,0:T(8,128)(2,1)S(1)} %get-tuple-element.33, ...), kind=kOutput, calls=%fused_computation.7 | convolution fusion | flops 839909376 | bytes 66191360 | tf_op jit(solution)/shard_map/dot_general | solution.py:56
  258.8 4.3 slice_bitcast_fusion.6
  263.1 4.5 fusion.28
  267.6 4.7 fusion.25
  272.3 4.6 fusion.22
  276.9 4.6 fusion.19
  281.5 4.6 fusion.16
  286.1 4.6 fusion.13
  290.7 4.6 fusion.7
  295.3 4.6 fusion.10
  299.9 27.1 %fusion.164 = (bf16[1,6,34,34,256]{4,2,1,3,0:T(8,128)(2,1)}, f32[1,6,34,34,256]{4,2,1,3,0:T(8,128)}) fusion(bf16[3,3,256,256]{3,2,1,0:T(8,128)(2,1)} %get-tuple-element.47, bf16[1,6,32,32,256]{4,2,1,3,0:T(8,128)(2,1)S(1)} %get-tuple-element.12, f32[6,34,34,256]{3,1,0,2:T(8,128)} %fusion.28, f32[6,34,34,256]{3,1,0,2:T(8,128)} %fusion.25, ...), kind=kOutput, calls=%fused_computation.247 | convolution fusion | flops 925095936 | bytes 80777216 | tf_op jit(solution)/shard_map/dot_general | solution.py:93
  340.0 6.4 %convert_add_fusion = f32[1,6,32,32,256]{4,2,1,3,0:T(8,128)S(1)} fusion(f32[1,6,34,34,256]{4,2,1,3,0:T(8,128)} %get-tuple-element.65, bf16[1,6,32,32,256]{4,3,2,1,0:T(8,128)(2,1)} %param.6), kind=kLoop, calls=%fused_computation.4 | loop fusion | flops 3145728 | bytes 15728640 | tf_op jit(solution)/shard_map/add | solution.py:161
  357.5 13.4 %all-gather.11.cloned.1.call-done = bf16[1,24,4,32,256]{4,3,1,2,0:T(8,128)(2,1)} async-done(((bf16[1,6,4,32,256]{4,3,1,2,0:T(8,128)(2,1)}), bf16[1,24,4,32,256]{4,3,1,2,0:T(8,128)(2,1)}) %all-gather.11.cloned.1.call-update) | async-done | bytes 1572880 | tf_op jit(solution)/shard_map/all_gather | solution.py:33
  405.4 5.4 %reduce-scatter.5.cloned.1.call-done = f32[3,3,32,256]{3,2,1,0:T(8,128)} async-done(((f32[3,3,256,256]{3,2,1,0:T(8,128)}), f32[3,3,32,256]{3,2,1,0:T(8,128)}) %reduce-scatter.5.cloned.1.call-update) | async-done | bytes 294928 | tf_op jit(solution)/shard_map/reduce_scatter | solution.py:137
  410.8 38.1 %reduce-scatter.3.cloned.1.call-done = f32[3,3,32,256]{3,2,1,0:T(8,128)} async-done(((f32[3,3,256,256]{3,2,1,0:T(8,128)}), f32[3,3,32,256]{3,2,1,0:T(8,128)}) %reduce-scatter.3.cloned.1.call-update) | async-done | bytes 294928 | tf_op jit(solution)/shard_map/reduce_scatter | solution.py:137
  452.5 44.4 %all-reduce.4.cloned.1.call-done = (f32[3,3,32,256]{3,2,1,0:T(8,128)}, f32[3,3,32,256]{3,2,1,0:T(8,128)}) async-done(((f32[3,3,32,256]{3,2,1,0:T(8,128)}, f32[3,3,32,256]{3,2,1,0:T(8,128)}), (f32[3,3,32,256]{3,2,1,0:T(8,128)}, f32[3,3,32,256]{3,2,1,0:T(8,128)})) %all-reduce.4.cloned.1.call-update) | async-done | bytes 589840 | tf_op jit(solution)/shard_map/psum | solution.py:136
  (191 shorter events, 129.6 us)
Async XLA Ops:
  7.2 3.9 copy-start.4
  7.2 5.6 %copy-start.40 = (s32[6,4,3]{0,1,2:T(4,128)S(1)}, s32[6,4,3]{0,1,2:T(4,128)}, u32[]{:S(2)}) copy-start(s32[6,4,3]{0,1,2:T(4,128)} %param.7) | copy-start | bytes 868
  7.2 38.5 %all-gather.5.cloned.1.call-start = ((), (), s32[]{:S(2)}) async-start(), calls=%async_computation.2 | async-start | bytes 1966080 | tf_op jit(solution)/shard_map/all_gather | solution.py:28
  11.9 66.8 %all-gather.7.cloned.1.call-start = ((), (), s32[]{:S(2)}) async-start(), calls=%async_computation.3 | async-start | bytes 2654208 | tf_op jit(solution)/shard_map/all_gather | solution.py:141
  12.7 173.3 %all-gather.9.cloned.1.call-start = ((), (), s32[]{:S(2)}) async-start(), calls=%async_computation.4 | async-start | bytes 1966080 | tf_op jit(solution)/shard_map/all_gather | solution.py:28
  81.7 6.2 %copy-start.17 = (bf16[6,32,32,256]{3,2,1,0:T(8,128)(2,1)S(1)}, bf16[6,32,32,256]{3,2,1,0:T(8,128)(2,1)}, u32[]{:S(2)}) copy-start(bf16[6,32,32,256]{3,2,1,0:T(8,128)(2,1)} %get-tuple-element.29) | copy-start | bytes 9437188
  88.0 6.2 %copy-start.16 = (bf16[6,32,32,256]{3,2,1,0:T(8,128)(2,1)S(1)}, bf16[6,32,32,256]{3,2,1,0:T(8,128)(2,1)}, u32[]{:S(2)}) copy-start(bf16[6,32,32,256]{3,2,1,0:T(8,128)(2,1)} %get-tuple-element.27) | copy-start | bytes 9437188
  94.2 6.3 %copy-start.21 = (bf16[6,32,32,256]{3,2,1,0:T(8,128)(2,1)S(1)}, bf16[6,32,32,256]{3,2,1,0:T(8,128)(2,1)}, u32[]{:S(2)}) copy-start(bf16[6,32,32,256]{3,2,1,0:T(8,128)(2,1)} %get-tuple-element.41) | copy-start | bytes 9437188
  106.8 6.3 %copy-start.19 = (bf16[6,32,32,256]{3,2,1,0:T(8,128)(2,1)S(1)}, bf16[6,32,32,256]{3,2,1,0:T(8,128)(2,1)}, u32[]{:S(2)}) copy-start(bf16[6,32,32,256]{3,2,1,0:T(8,128)(2,1)} %get-tuple-element.40) | copy-start | bytes 9437188
  113.1 6.3 %copy-start.15 = (bf16[6,32,32,256]{3,2,1,0:T(8,128)(2,1)S(1)}, bf16[6,32,32,256]{3,2,1,0:T(8,128)(2,1)}, u32[]{:S(2)}) copy-start(bf16[6,32,32,256]{3,2,1,0:T(8,128)(2,1)} %get-tuple-element.67) | copy-start | bytes 9437188
  119.3 6.7 %copy-start.14 = (bf16[6,32,32,256]{3,2,1,0:T(8,128)(2,1)S(1)}, bf16[6,32,32,256]{3,2,1,0:T(8,128)(2,1)}, u32[]{:S(2)}) copy-start(bf16[6,32,32,256]{3,2,1,0:T(8,128)(2,1)} %get-tuple-element.66) | copy-start | bytes 9437188
  126.0 6.2 %copy-start.5 = (bf16[1,6,32,32,256]{4,3,2,1,0:T(8,128)(2,1)S(1)}, bf16[1,6,32,32,256]{4,3,2,1,0:T(8,128)(2,1)}, u32[]{:S(2)}) copy-start(bf16[1,6,32,32,256]{4,3,2,1,0:T(8,128)(2,1)} %param.4) | copy-start | bytes 9437188
  126.0 6.2 %copy-start.12 = (bf16[6,32,32,256]{3,2,1,0:T(8,128)(2,1)S(1)}, bf16[6,32,32,256]{3,2,1,0:T(8,128)(2,1)}, u32[]{:S(2)}) copy-start(bf16[6,32,32,256]{3,2,1,0:T(8,128)(2,1)} %get-tuple-element.68) | copy-start | bytes 9437188
  154.3 48.6 %copy-start.2 = (bf16[1,6,32,32,256]{4,2,1,3,0:T(8,128)(2,1)}, bf16[1,6,32,32,256]{4,2,1,3,0:T(8,128)(2,1)S(1)}, u32[]{:S(2)}) copy-start(bf16[1,6,32,32,256]{4,2,1,3,0:T(8,128)(2,1)S(1)} %get-tuple-element.62) | copy-start | bytes 9437188
  155.8 215.2 %all-gather.11.cloned.1.call-start = ((), (), s32[]{:S(2)}) async-start(), calls=%async_computation.5 | async-start | bytes 1966080 | tf_op jit(solution)/shard_map/all_gather | solution.py:33
  195.3 15.9 %copy-start = (bf16[1,6,33,34,256]{4,2,1,3,0:T(8,128)(2,1)}, bf16[1,6,33,34,256]{4,2,1,3,0:T(8,128)(2,1)S(1)}, u32[]{:S(2)}) copy-start(bf16[1,6,33,34,256]{4,2,1,3,0:T(8,128)(2,1)S(1)} %get-tuple-element.32) | copy-start | bytes 10340356
  203.4 18.5 %copy-start.25 = (bf16[6,32,32,256]{3,1,0,2:T(8,128)(2,1)}, bf16[6,32,32,256]{3,1,0,2:T(8,128)(2,1)S(1)}, u32[]{:S(2)}) copy-start(bf16[6,32,32,256]{3,1,0,2:T(8,128)(2,1)S(1)} %get-tuple-element.35) | copy-start | bytes 9437188
  203.4 22.1 %copy-start.23 = (bf16[6,32,32,256]{3,1,0,2:T(8,128)(2,1)}, bf16[6,32,32,256]{3,1,0,2:T(8,128)(2,1)S(1)}, u32[]{:S(2)}) copy-start(bf16[6,32,32,256]{3,1,0,2:T(8,128)(2,1)S(1)} %get-tuple-element.34) | copy-start | bytes 9437188
  258.8 4.3 copy-start.27
  339.9 70.8 %reduce-scatter.5.cloned.1.call-start = ((), (), s32[]{:S(2)}) async-start(), calls=%async_computation.7 | async-start | bytes 2654208 | tf_op jit(solution)/shard_map/reduce_scatter | solution.py:137
  346.4 4.6 copy-start.11
  346.4 4.6 copy-start.37
  346.4 4.6 copy-start.38
  346.4 4.6 copy-start.39
  346.4 4.7 copy-start.33
  346.4 4.7 copy-start.34
  346.4 4.7 copy-start.35
  357.4 19.9 %slice-start = ((s8[6291456]{0:T(1024)(128)(4,1)}), s8[2097152]{0:T(1024)(128)(4,1)S(1)}, s32[]{:S(2)}) async-start(s8[6291456]{0:T(1024)(128)(4,1)} %bitcast.433), calls=%async_computation.9 | async-start | bytes 4194304
  357.5 91.4 %reduce-scatter.3.cloned.1.call-start = ((), (), s32[]{:S(2)}) async-start(), calls=%async_computation.6 | async-start | bytes 2654208 | tf_op jit(solution)/shard_map/reduce_scatter | solution.py:137
  373.5 3.9 slice-start.1
  403.8 45.2 %copy-start.13 = (bf16[1,6,32,32,256]{4,2,1,3,0:T(8,128)(2,1)S(1)}, bf16[1,6,32,32,256]{4,2,1,3,0:T(8,128)(2,1)}, u32[]{:S(2)}) copy-start(bf16[1,6,32,32,256]{4,2,1,3,0:T(8,128)(2,1)} %get-tuple-element.13) | copy-start | bytes 9437188
  405.3 91.5 %all-reduce.4.cloned.1.call-start = ((), (), s32[]{:S(2)}) async-start(), calls=%async_computation.8 | async-start | bytes 1179648 | tf_op jit(solution)/shard_map/psum | solution.py:136
  (20 other events, 49.2 us)
Sparse Core Ops, SparseCore 0:
  12.0 33.5 all-gather.4
  47.2 31.4 all-gather.6
  155.9 30.0 all-gather.8
  340.0 30.8 all-gather.10
  373.7 37.0 reduce-scatter.4
  412.9 35.9 reduce-scatter.2
  451.9 44.8 all-reduce.3
where the time goes:
time: 513 us; the launch traced here: 506 us
  matrix products  228 us (44%)
  waiting for transfers between devices  163 us (32%)
  local copies, waits for them, and re-layouts  60.8 us (12%)
  other arithmetic  38.2 us (7%)
  between operations  15.1 us (3%)
    dot_general x18, matrix products, convolve(): jnp.dot(patches, kernel[row_off, col_off], preferred_element_type=jnp.flo...  125 us
    dot_general x9, matrix products, input_grad(): lax.dot_general(window, kernel[row_off, col_off], (((1,), (1,)), ((), ())...  63.9 us
    all_gather x2, waiting for transfers between devices, neighbor_rims(): lax.all_gather(edge_strips(tile_field), 'space', axis=1, tiled=True)  58.4 us
    psum x1, waiting for transfers between devices, reduce_grad(): space_total = lax.psum(partial_value, 'space')  44.4 us
    reduce_scatter x2, waiting for transfers between devices, reduce_grad(): return lax.psum_scatter(space_total, 'dp', scatter_dimension=2, tiled=True)  43.5 us
    dot_general x18, matrix products, weight_grad(): lax.dot_general(patches, flat_grad, (((0,), (0,)), ((), ())), preferred_e...  39.5 us
    dot_general x3, local copies, waits for them, and re-layouts, convolve(): jnp.dot(patches, kernel[row_off, col_off], preferred_element_type=jnp.flo...  22 us
    unnamed x97, local copies, waits for them, and re-layouts  15.4 us
  transfers between devices with their start and end apart: 7, of which 7 were waited for; matrix products, arithmetic and copies ran while one was open for 16% of the time, Pallas kernels for 0%

commit v1 on v0

v1 whole, which is shorter than its diff:
```python
import functools

import jax
import jax.numpy as jnp
from jax import lax
from jax.experimental import pallas as pl
from jax.experimental.pallas import tpu as pltpu
from jax.sharding import PartitionSpec as P

LAYERS = 2
F32 = jnp.float32
BF16 = jnp.bfloat16


def edge_strips(field):
    return jnp.stack(
        [field[:, 0], field[:, -1], field[:, :, 0], field[:, :, -1]], axis=1
    )


def orient(strips, adjacency):
    selected = strips[adjacency[:, :, 0], adjacency[:, :, 1]]
    flipped = (adjacency[:, :, 2] == 1)[:, :, None, None]
    return jnp.where(flipped, selected[:, :, ::-1], selected)


def exchange(strips, adjacency):
    return orient(lax.all_gather(strips, "space", axis=0, tiled=True), adjacency)


def fill(x3, field, rims):
    s, _, c = field.shape
    col = lax.broadcasted_iota(jnp.int32, (s, s, c), 1)
    wide = field.astype(F32)
    if rims is None:
        left = right = jnp.zeros((1, 1, 1), F32)
    else:
        left = rims[2].astype(F32)[:, None, :]
        right = rims[3].astype(F32)[:, None, :]
    x3[1 : s + 1, :, c : 2 * c] = field
    x3[1 : s + 1, :, 0:c] = jnp.where(col == 0, left, pltpu.roll(wide, 1, 1)).astype(BF16)
    x3[1 : s + 1, :, 2 * c :] = jnp.where(
        col == s - 1, right, pltpu.roll(wide, s - 1, 1)
    ).astype(BF16)
    rc = lax.broadcasted_iota(jnp.int32, (s, c), 0)
    for row, edge in ((0, 0), (s + 1, 1)):
        if rims is None:
            x3[row] = jnp.zeros((s, 3 * c), BF16)
        else:
            line = rims[edge].astype(F32)
            x3[row, :, c : 2 * c] = rims[edge]
            x3[row, :, 0:c] = jnp.where(rc == 0, 0.0, pltpu.roll(line, 1, 0)).astype(BF16)
            x3[row, :, 2 * c :] = jnp.where(
                rc == s - 1, 0.0, pltpu.roll(line, s - 1, 0)
            ).astype(BF16)


def conv(x3, w):
    s = x3.shape[1]
    k = x3.shape[2]
    total = None
    for p in range(3):
        part = jnp.dot(
            x3[p : p + s].reshape(s * s, k), w[p], preferred_element_type=F32
        )
        total = part if total is None else total + part
    return total.reshape(s, s, -1)


def wgrad_add(acc, x3, grad):
    s = x3.shape[1]
    k = x3.shape[2]
    flipped = grad.reshape(s * s, -1).T
    for p in range(3):
        acc[p] += jnp.dot(
            flipped, x3[p : p + s].reshape(s * s, k), preferred_element_type=F32
        )


def k_first(x, rims, w, state, slope, x3):
    fill(x3, x[0], rims[0])
    v = conv(x3, w)
    sg = jax.nn.sigmoid(v)
    state[0] = (x[0].astype(F32) + v * sg).astype(BF16)
    slope[0] = (sg * (1.0 + v * (1.0 - sg))).astype(slope.dtype)


def k_last(x, rims, w, wt, cot, state, grad, rim_grad, x3, g3):
    s = x.shape[1]
    c = x.shape[3]
    fill(x3, x[0], rims[0])
    v = conv(x3, w)
    sg = jax.nn.sigmoid(v)
    state[0] = (x[0].astype(F32) + v * sg).astype(BF16)
    g32 = cot[0].astype(F32) * (sg * (1.0 + v * (1.0 - sg)))
    g = g32.astype(BF16)
    grad[0] = g
    fill(g3, g, None)
    rim_grad[0, 0] = jnp.dot(g3[1], wt[2], preferred_element_type=F32).astype(BF16)
    rim_grad[0, 1] = jnp.dot(g3[s], wt[0], preferred_element_type=F32).astype(BF16)
    for edge, col, q in ((2, 0, 2), (3, s - 1, 0)):
        line = jnp.concatenate(
            [g3[p : p + s, :, c : 2 * c].astype(F32)[:, col, :] for p in range(3)], axis=1
        ).astype(BF16)
        weight = jnp.concatenate([wt[p, q * c : (q + 1) * c] for p in range(3)], axis=0)
        rim_grad[0, edge] = jnp.dot(line, weight, preferred_element_type=F32).astype(BF16)


def finish_wgrad(acc, out):
    @pl.when(pl.program_id(0) == pl.num_programs(0) - 1)
    def _():
        for p in range(3):
            out[p] = acc[p].T


def k_back(x, rims, g, wt, cot, up, dw, x3, g3, acc):
    @pl.when(pl.program_id(0) == 0)
    def _():
        acc[...] = jnp.zeros_like(acc)

    fill(x3, x[0], rims[0])
    wgrad_add(acc, x3, g[0])
    fill(g3, g[0], None)
    up[0] = cot[0].astype(F32) + conv(g3, wt)
    finish_wgrad(acc, dw)


def k_tail(x, rims, up, back, slope, dw, x3, acc):
    @pl.when(pl.program_id(0) == 0)
    def _():
        acc[...] = jnp.zeros_like(acc)

    s = x.shape[1]
    fill(x3, x[0], rims[0])
    u = up[0]
    row = lax.broadcasted_iota(jnp.int32, u.shape, 0)
    col = lax.broadcasted_iota(jnp.int32, u.shape, 1)
    r = back[0].astype(F32)
    u = u + jnp.where(row == 0, r[0][None], 0.0) + jnp.where(row == s - 1, r[1][None], 0.0)
    u = u + jnp.where(col == 0, r[2][:, None, :], 0.0)
    u = u + jnp.where(col == s - 1, r[3][:, None, :], 0.0)
    g = (u * slope[0].astype(F32)).astype(BF16)
    wgrad_add(acc, x3, g)
    finish_wgrad(acc, dw)


def reduce_grad(dw, c):
    dw = dw.reshape(3, 3, c, c)
    part = lax.psum_scatter(dw, "dp", scatter_dimension=2, tiled=True)
    return lax.psum(part, "space")


def per_device(inputs, kernels, cotangent, adjacency):
    _, t, s, _, c = inputs.shape
    x0 = inputs[0]
    cot = cotangent[0]
    weights = [lax.all_gather(kernels[l], "dp", axis=2, tiled=True) for l in range(2)]
    w1 = weights[0].reshape(3, 3 * c, c)
    w2 = weights[1].reshape(3, 3 * c, c)
    wt = jnp.transpose(weights[1][::-1, ::-1], (0, 1, 3, 2)).reshape(3, 3 * c, c)

    tile = pl.BlockSpec((1, s, s, c), lambda i: (i, 0, 0, 0))
    rim = pl.BlockSpec((1, 4, s, c), lambda i: (i, 0, 0, 0))
    wsp = pl.BlockSpec((3, 3 * c, c), lambda i: (0, 0, 0), pipeline_mode=pl.Buffered(1))
    field = lambda dt: jax.ShapeDtypeStruct((t, s, s, c), dt)
    dws = jax.ShapeDtypeStruct((3, 3 * c, c), F32)
    x3s = pltpu.VMEM((s + 2, s, 3 * c), BF16)
    accs = pltpu.VMEM((3, c, 3 * c), F32)
    flops = 2 * t * s * s * c * c * 9
    call = lambda body, nf, ins, outs, shapes, scratch: pl.pallas_call(
        body,
        grid=(t,),
        in_specs=ins,
        out_specs=outs,
        out_shape=shapes,
        scratch_shapes=scratch,
        compiler_params=pltpu.CompilerParams(vmem_limit_bytes=60 << 20),
        cost_estimate=pl.CostEstimate(
            flops=nf * flops, bytes_accessed=12 << 20, transcendentals=0
        ),
    )
    rims0 = exchange(edge_strips(x0), adjacency)
    state1, slope1 = call(
        k_first, 1, [tile, rim, wsp], [tile, tile], [field(BF16), field(BF16)], [x3s]
    )(x0, rims0, w1)
    rims1 = exchange(edge_strips(state1), adjacency)
    state2, g2, rg = call(
        k_last,
        1,
        [tile, rim, wsp, wsp, tile],
        [tile, tile, rim],
        [field(BF16), field(BF16), jax.ShapeDtypeStruct((t, 4, s, c), BF16)],
        [x3s, x3s],
    )(state1, rims1, w2, wt, cot)
    back = exchange(rg, adjacency)
    up, dw2 = call(
        k_back, 2, [tile, rim, tile, wsp, tile], [tile, wsp], [field(F32), dws], [x3s, x3s, accs]
    )(state1, rims1, g2, wt, cot)
    dw2r = reduce_grad(dw2, c)
    dw1 = call(k_tail, 1, [tile, rim, tile, rim, tile], wsp, dws, [x3s, accs])(
        x0, rims0, up, back, slope1
    )
    dw1r = reduce_grad(dw1, c)
    return state2[None], jnp.stack([dw1r, dw2r])


def solution(mesh):
    in_specs = (
        P("dp", "space", None, None, None),
        P(None, None, None, "dp", None),
        P("dp", "space", None, None, None),
        P("space", None, None),
    )
    out_specs = (P("dp", "space", None, None, None), P(None, None, None, "dp", None))
    return jax.shard_map(
        per_device, mesh=mesh, in_specs=in_specs, out_specs=out_specs, check_vma=False
    )
```

time: 513 us -> 311 us (0.61); the launches traced: 506 us -> 311 us
  matrix products: 228 us -> 0 us
  Pallas kernels: 0 us -> 62.5 us
  waiting for transfers between devices: 163 us -> 211 us
  local copies, waits for them, and re-layouts: 60.8 us -> 16.5 us
  other arithmetic: 38.2 us -> 6.1 us
    dot_general x45 -> x0, matrix products: 228 us -> none  [the longest x18 125 us: convolve(): jnp.dot(patches, kernel[row_off, col_off], preferred_element_type=jnp.flo...]
    pallas_call x0 -> x4, Pallas kernels: none -> 62.5 us  [the longest x1 20.7 us: per_device(): call(k_back, 2, [tile, rim, tile, wsp, tile], [tile, wsp], [field(F32), d...]
    all_gather x4 -> x5, waiting for transfers between devices: 74.5 us -> 102 us  [the longest x3 71.9 us: exchange(): lax.all_gather(strips, 'space', axis=0, tiled=True)]
    dot_general x3 -> x0, local copies, waits for them, and re-layouts: 22 us -> none  [convolve(): jnp.dot(patches, kernel[row_off, col_off], preferred_element_type=jnp.flo...]
    reduce_scatter x2, waiting for transfers between devices: 43.5 us -> 60.3 us  [reduce_grad(): part = lax.psum_scatter(dw, 'dp', scatter_dimension=2, tiled=True)]
    unnamed x97 -> x6, local copies, waits for them, and re-layouts: 15.4 us -> 0.04 us
    concatenate x5 -> x1, other arithmetic: 10.1 us -> 0.01 us  [orient(): selected = strips[adjacency[:, :, 0], adjacency[:, :, 1]]]
    add x2 -> x0, other arithmetic: 8.98 us -> none  [the longest x1 6.41 us: per_device(): upstream = add_rim(upstream + pad_grad[:, :, 1:-1, 1:-1], returned)]
  transfers between devices with their start and end apart: 7 -> 8, of which waited for: 7 -> 8; matrix products, arithmetic and copies ran while one was open for 16% -> 4% of each run, Pallas kernels for 0% -> 15%
where the time goes in v1:
time: 311 us
  waiting for transfers between devices  211 us (68%)
  Pallas kernels  62.5 us (20%)
  local copies, waits for them, and re-layouts  16.5 us (5%)
  between operations  14.3 us (5%)
  other arithmetic  6.1 us (2%)
    all_gather x3, waiting for transfers between devices, exchange(): lax.all_gather(strips, 'space', axis=0, tiled=True)  71.9 us
    reduce_scatter x2, waiting for transfers between devices, reduce_grad(): part = lax.psum_scatter(dw, 'dp', scatter_dimension=2, tiled=True)  60.3 us
    psum x1, waiting for transfers between devices, reduce_grad(): return lax.psum(part, 'space')  47.9 us
    all_gather x2, waiting for transfers between devices, per_device(): lax.all_gather(kernels[l], 'dp', axis=2, tiled=True)  30.4 us
    pallas_call x1, Pallas kernels, per_device(): call(k_back, 2, [tile, rim, tile, wsp, tile], [tile, wsp], [field(F32), d...  20.7 us
    pallas_call x1, Pallas kernels, per_device(): call(k_last, 1, [tile, rim, wsp, wsp, tile], [tile, tile, rim], [field(BF...  16.2 us
    pallas_call x1, Pallas kernels, per_device(): call(k_tail, 1, [tile, rim, tile, rim, tile], wsp, dws, [x3s, accs])  13.9 us
    pallas_call x1, Pallas kernels, per_device(): call(k_first, 1, [tile, rim, wsp], [tile, tile], [field(BF16), field(BF16...  11.8 us
  transfers between devices with their start and end apart: 8, of which 8 were waited for; matrix products, arithmetic and copies ran while one was open for 4% of the time, Pallas kernels for 15%

profile of v1, /device:TPU:0, one launch (start us, length us, event | category | flops | bytes accessed | tf_op | source)
XLA Modules:
  0.0 311.0 jit_solution(553619976892402182)
XLA Ops:
  7.2 1.0 fusion.8
  8.2 1.7 fusion.9
  10.0 0.8 pad_maximum_fusion.1
  10.9 0.7 fusion.10
  11.7 0.7 all-gather.16.cloned.1.call-update
  12.7 31.8 %all-gather.8.cloned.1.call-done = bf16[24,4,32,256]{3,2,1,0:T(8,128)(2,1)} async-done(((bf16[6,4,32,256]{3,2,1,0:T(8,128)(2,1)}), bf16[24,4,32,256]{3,2,1,0:T(8,128)(2,1)}) %all-gather.8.cloned.1.call-update) | async-done | bytes 1572880 | tf_op jit(solution)/shard_map/all_gather | solution.py:28
  44.6 2.1 gather_fusion
  46.6 0.3 rev.12
  46.9 0.9 broadcast_select_fusion.2.rims
  47.8 21.8 %all-gather.14.cloned.1.call-done = bf16[1,3,3,256,256]{4,3,2,1,0:T(8,128)(2,1)} async-done(((bf16[1,3,3,32,256]{4,3,2,1,0:T(8,128)(2,1)}), bf16[1,3,3,256,256]{4,3,2,1,0:T(8,128)(2,1)}) %all-gather.14.cloned.1.call-update) | async-done | bytes 1179664 | tf_op jit(solution)/shard_map/all_gather | solution.py:157
  69.5 11.8 %shard_map.59 = (bf16[6,32,32,256]{3,2,1,0:T(8,128)(2,1)}, bf16[6,32,32,256]{3,2,1,0:T(8,128)(2,1)}) custom-call(bf16[6,32,32,256]{3,2,1,0:T(8,128)(2,1)} %bitcast.56, bf16[6,4,32,256]{3,2,1,0:T(8,128)(2,1)} %broadcast_select_fusion.2.rims, bf16[3,768,256]{2,1,0:T(8,128)(2,1)} %bitcast.60), custom_call_target="tpu_custom_call" | custom-call | flops 7247757312 | bytes 12582912 | tf_op jit(solution)/shard_map/pallas_call | solution.py:183
  81.3 1.7 fusion.7
  83.1 1.0 fusion.6
  84.1 0.8 pad_maximum_fusion.2
  85.0 8.7 %all-gather.16.cloned.1.call-done = bf16[1,3,3,256,256]{4,3,2,1,0:T(8,128)(2,1)} async-done(((bf16[1,3,3,32,256]{4,3,2,1,0:T(8,128)(2,1)}), bf16[1,3,3,256,256]{4,3,2,1,0:T(8,128)(2,1)}) %all-gather.16.cloned.1.call-update) | async-done | bytes 1179664 | tf_op jit(solution)/shard_map/all_gather | solution.py:157
  93.6 1.3 reverse_bitcast_fusion
  95.0 1.5 copy.35
  96.5 29.9 %all-gather.10.cloned.1.call-done = bf16[24,4,32,256]{3,2,1,0:T(8,128)(2,1)} async-done(((bf16[6,4,32,256]{3,2,1,0:T(8,128)(2,1)}), bf16[24,4,32,256]{3,2,1,0:T(8,128)(2,1)}) %all-gather.10.cloned.1.call-update) | async-done | bytes 1572880 | tf_op jit(solution)/shard_map/all_gather | solution.py:28
  126.4 2.1 gather_fusion.1
  128.5 0.3 rev.13
  128.8 0.9 broadcast_select_fusion.1.rims
  129.6 16.2 %shard_map.60 = (bf16[6,32,32,256]{3,2,1,0:T(8,128)(2,1)}, bf16[6,32,32,256]{3,2,1,0:T(8,128)(2,1)}, bf16[6,4,32,256]{3,2,1,0:T(8,128)(2,1)}) custom-call(bf16[6,32,32,256]{3,2,1,0:T(8,128)(2,1)} %get-tuple-element.9.x, bf16[6,4,32,256]{3,2,1,0:T(8,128)(2,1)} %broadcast_select_fusion.1.rims, bf16[3,768,256]{2,1,0:T(8,128)(2,1)} %bitcast.47, ...), custom_call_target="tpu_custom_call" | custom-call | flops 7247757312 | bytes 12582912 | tf_op jit(solution)/shard_map/pallas_call | solution.py:187
  145.9 20.7 %shard_map.61 = (f32[6,32,32,256]{3,2,1,0:T(8,128)}, f32[3,768,256]{2,1,0:T(8,128)}) custom-call(bf16[6,32,32,256]{3,2,1,0:T(8,128)(2,1)} %get-tuple-element.9.x, bf16[6,4,32,256]{3,2,1,0:T(8,128)(2,1)} %broadcast_select_fusion.1.rims, bf16[6,32,32,256]{3,2,1,0:T(8,128)(2,1)} %get-tuple-element.11.g, bf16[3,768,256]{2,1,0:T(8,128)(2,1)} %bitcast.49, ...), custom_call_target="tpu_custom_call" | custom-call | flops 14495514624 | bytes 12582912 | tf_op jit(solution)/shard_map/pallas_call | solution.py:196
  166.6 10.2 %all-gather.12.cloned.1.call-done = bf16[24,4,32,256]{3,2,1,0:T(8,128)(2,1)} async-done(((bf16[6,4,32,256]{3,2,1,0:T(8,128)(2,1)}), bf16[24,4,32,256]{3,2,1,0:T(8,128)(2,1)}) %all-gather.12.cloned.1.call-update) | async-done | bytes 1572880 | tf_op jit(solution)/shard_map/all_gather | solution.py:28
  176.8 2.1 gather_fusion.2
  178.9 0.3 rev.15
  179.2 0.9 broadcast_select_fusion.back
  180.1 13.9 %shard_map.62 = f32[3,768,256]{2,1,0:T(8,128)} custom-call(bf16[6,32,32,256]{3,2,1,0:T(8,128)(2,1)} %bitcast.57, bf16[6,4,32,256]{3,2,1,0:T(8,128)(2,1)} %broadcast_select_fusion.2.rims, f32[6,32,32,256]{3,2,1,0:T(8,128)} %get-tuple-element.12.up, bf16[6,4,32,256]{3,2,1,0:T(8,128)(2,1)} %broadcast_select_fusion.back, ...), custom_call_target="tpu_custom_call" | custom-call | flops 7247757312 | bytes 12582912 | tf_op jit(solution)/shard_map/pallas_call | solution.py:200
  194.1 22.0 %reduce-scatter.5.cloned.1.call-done = f32[3,3,32,256]{3,2,1,0:T(8,128)} async-done(((f32[3,3,256,256]{3,2,1,0:T(8,128)}), f32[3,3,32,256]{3,2,1,0:T(8,128)}) %reduce-scatter.5.cloned.1.call-update) | async-done | bytes 294928 | tf_op jit(solution)/shard_map/reduce_scatter | solution.py:149
  216.1 38.3 %reduce-scatter.3.cloned.1.call-done = f32[3,3,32,256]{3,2,1,0:T(8,128)} async-done(((f32[3,3,256,256]{3,2,1,0:T(8,128)}), f32[3,3,32,256]{3,2,1,0:T(8,128)}) %reduce-scatter.3.cloned.1.call-update) | async-done | bytes 294928 | tf_op jit(solution)/shard_map/reduce_scatter | solution.py:149
  254.4 47.9 %all-reduce.3.cloned.1.call-done = (f32[1,3,3,32,256]{4,3,2,1,0:T(8,128)}, f32[1,3,3,32,256]{4,3,2,1,0:T(8,128)}) async-done(((f32[1,3,3,32,256]{4,3,2,1,0:T(8,128)}, f32[1,3,3,32,256]{4,3,2,1,0:T(8,128)}), (f32[1,3,3,32,256]{4,3,2,1,0:T(8,128)}, f32[1,3,3,32,256]{4,3,2,1,0:T(8,128)})) %all-reduce.3.cloned.1.call-update) | async-done | bytes 589840 | tf_op jit(solution)/shard_map/psum | solution.py:150
  302.3 1.9 pad_maximum_fusion
  (27 shorter events, 0.8 us)
Async XLA Ops:
  7.2 3.7 %copy-start = (bf16[2,3,3,32,256]{4,3,2,1,0:T(8,128)(2,1)S(1)}, bf16[2,3,3,32,256]{4,3,2,1,0:T(8,128)(2,1)}, u32[]{:S(2)}) copy-start(bf16[2,3,3,32,256]{4,3,2,1,0:T(8,128)(2,1)} %param.5) | copy-start | bytes 884740
  7.2 5.3 %copy-start.1 = (s32[6,4,3]{0,1,2:T(4,128)S(1)}, s32[6,4,3]{0,1,2:T(4,128)}, u32[]{:S(2)}) copy-start(s32[6,4,3]{0,1,2:T(4,128)} %param.7) | copy-start | bytes 868
  7.2 37.4 %all-gather.8.cloned.1.call-start = ((), (), s32[]{:S(2)}) async-start(), calls=%async_computation.2 | async-start | bytes 1966080 | tf_op jit(solution)/shard_map/all_gather | solution.py:28
  10.8 58.7 %all-gather.14.cloned.1.call-start = ((), (), s32[]{:S(2)}) async-start(), calls=%async_computation.7 | async-start | bytes 1327104 | tf_op jit(solution)/shard_map/all_gather | solution.py:157
  11.6 82.0 %all-gather.16.cloned.1.call-start = ((), (), s32[]{:S(2)}) async-start(), calls=%async_computation.8 | async-start | bytes 1327104 | tf_op jit(solution)/shard_map/all_gather | solution.py:157
  12.4 114.0 %all-gather.10.cloned.1.call-start = ((), (), s32[]{:S(2)}) async-start(), calls=%async_computation.3 | async-start | bytes 1966080 | tf_op jit(solution)/shard_map/all_gather | solution.py:28
  84.9 91.9 %all-gather.12.cloned.1.call-start = ((), (), s32[]{:S(2)}) async-start(), calls=%async_computation.4 | async-start | bytes 1966080 | tf_op jit(solution)/shard_map/all_gather | solution.py:28
  145.8 70.2 %reduce-scatter.5.cloned.1.call-start = ((), (), s32[]{:S(2)}) async-start(), calls=%async_computation.6 | async-start | bytes 2654208 | tf_op jit(solution)/shard_map/reduce_scatter | solution.py:149
  166.6 87.8 %reduce-scatter.3.cloned.1.call-start = ((), (), s32[]{:S(2)}) async-start(), calls=%async_computation.5 | async-start | bytes 2654208 | tf_op jit(solution)/shard_map/reduce_scatter | solution.py:149
  194.0 108.3 %all-reduce.3.cloned.1.call-start = ((), (), s32[]{:S(2)}) async-start(), calls=%async_computation.9 | async-start | bytes 1179648 | tf_op jit(solution)/shard_map/psum | solution.py:150
Sparse Core Ops, SparseCore 0:
  11.0 33.5 all-gather.7
  46.7 22.7 all-gather.13
  71.2 22.4 all-gather.15
  95.9 30.4 all-gather.9
  146.0 30.8 all-gather.11
  179.0 37.0 reduce-scatter.4
  218.4 35.9 reduce-scatter.2
  257.3 44.8 all-reduce.2

commit v2 on v1

--- a/solution.py
+++ b/solution.py
@@ -24,8 +24,12 @@
     return jnp.where(flipped, selected[:, :, ::-1], selected)
 
 
-def exchange(strips, adjacency):
-    return orient(lax.all_gather(strips, "space", axis=0, tiled=True), adjacency)
+def exchange(strips, adjacency, n_sp, cid):
+    if n_sp == 4:
+        every = swap_strips(strips, cid).reshape((-1,) + strips.shape[1:])
+    else:
+        every = lax.all_gather(strips, "space", axis=0, tiled=True)
+    return orient(every, adjacency)
 
 
 def fill(x3, field, rims):
@@ -109,8 +113,13 @@
 def finish_wgrad(acc, out):
     @pl.when(pl.program_id(0) == pl.num_programs(0) - 1)
     def _():
+        n, _, c = out.shape
+        depth = c // n
         for p in range(3):
-            out[p] = acc[p].T
+            for q in range(3):
+                tap = acc[p, :, q * c : (q + 1) * c].T.astype(out.dtype)
+                first = (3 * p + q) * depth
+                out[:, first : first + depth, :] = tap.reshape(n, depth, c)
 
 
 def k_back(x, rims, g, wt, cot, up, dw, x3, g3, acc):
@@ -144,17 +153,333 @@
     finish_wgrad(acc, dw)
 
 
-def reduce_grad(dw, c):
-    dw = dw.reshape(3, 3, c, c)
-    part = lax.psum_scatter(dw, "dp", scatter_dimension=2, tiled=True)
-    return lax.psum(part, "space")
-
-
-def per_device(inputs, kernels, cotangent, adjacency):
+def reduce_grads(dw1, dw2, n_dp, n_sp):
+    both = jnp.concatenate([dw1, dw2], axis=1)
+    n, rows, c = both.shape
+    if n_sp == 4:
+        total = sum_grads(n_dp, both, 3)
+    else:
+        part = lax.psum_scatter(both.astype(F32), "dp", scatter_dimension=0, tiled=True)
+        total = lax.psum(part, "space")
+    return total.reshape(LAYERS, 3, 3, c // n, c)
+
+
+def remote(src, dst, sems, i, who):
+    return pltpu.make_async_remote_copy(
+        src_ref=src,
+        dst_ref=dst,
+        send_sem=sems.at[0, i],
+        recv_sem=sems.at[1, i],
+        device_id=who,
+        device_id_type=pl.DeviceIdType.MESH,
+    )
+
+
+def square():
+    me = lax.axis_index("space")
+    xn = me + 1 - 2 * (me % 2)
+    yn = (me + 2) % 4
+    return me, xn, yn, (xn + 2) % 4
+
+
+def swap_start(src, out, sems):
+    me, xn, yn, _ = square()
+    h = src.shape[0] // 2
+    lo, hi = pl.ds(0, h), pl.ds(h, src.shape[0] - h)
+    copies = [
+        remote(src.at[lo], out.at[me, lo], sems, 0, {"space": xn}),
+        remote(src.at[hi], out.at[me, hi], sems, 1, {"space": yn}),
+        remote(src.at[hi], out.at[me, hi], sems, 2, {"space": xn}),
+        remote(src.at[lo], out.at[me, lo], sems, 3, {"space": yn}),
+    ]
+    for copy in copies:
+        copy.start()
+    return copies
+
+
+def swap_relay(copies, out, sems):
+    me, xn, yn, _ = square()
+    t = out.shape[1]
+    h = t // 2
+    lo, hi = pl.ds(0, h), pl.ds(h, t - h)
+    copies[0].wait_recv()
+    first = remote(out.at[xn, lo], out.at[xn, lo], sems, 4, {"space": yn})
+    first.start()
+    copies[1].wait_recv()
+    second = remote(out.at[yn, hi], out.at[yn, hi], sems, 5, {"space": xn})
+    second.start()
+    return copies + [first, second]
+
+
+def swap_end(copies):
+    for i, copy in enumerate(copies):
+        copy.wait_send()
+        if i >= 2:
+            copy.wait_recv()
+
+
+def greet(peers):
+    barrier = pltpu.get_barrier_semaphore()
+    for who in peers:
+        pl.semaphore_signal(
+            barrier, inc=1, device_id=who, device_id_type=pl.DeviceIdType.MESH
+        )
+    pl.semaphore_wait(barrier, len(peers))
+
+
+def c_swap(src, out, sems, own):
+    me, xn, yn, _ = square()
+    greet([{"space": xn}, {"space": yn}])
+    copies = swap_start(src, out, sems)
+    local = pltpu.make_async_copy(src, out.at[me], own)
+    local.start()
+    swap_end(swap_relay(copies, out, sems))
+    local.wait()
+
+
+def c_open(n_dp, w_in, src, w_out, out, sems, own, zs, ps):
+    me, xn, yn, _ = square()
+    line = n_dp // 2
+    dp = lax.axis_index("dp")
+    q, core = dp // 2, dp % 2
+    depth = w_in.shape[3]
+    layers = w_in.shape[0]
+    right = {"dp": ((q + 1) % line) * 2 + core}
+    left = {"dp": ((q + line - 1) % line) * 2 + core}
+    partner = {"dp": q * 2 + 1 - core}
+    greet([{"space": xn}, {"space": yn}, right, left, partner])
+    copies = swap_start(src, out, sems)
+    local = pltpu.make_async_copy(src, out.at[me], own.at[0])
+    local.start()
+
+    def slot(l, o, c):
+        return w_out.at[l, :, :, pl.ds(pl.multiple_of((o * 2 + c) * depth, depth), depth), :]
+
+    keep = pltpu.make_async_copy(
+        w_in, w_out.at[:, :, :, pl.ds(pl.multiple_of(dp * depth, depth), depth), :], own.at[1]
+    )
+    keep.start()
+
+    def move(l, o, who, sm, i, first):
+        ref = w_in.at[l] if first else slot(l, o, core)
+        return remote(ref, slot(l, o, core), sm, i, who)
+
+    def zi(l, s, way):
+        return (l * line + s) * 2 + way
+
+    def forward(l, s, way, o, first):
+        who = right if way == 0 else left
+        ok = (q + 1 < line) if way == 0 else (q > 0)
+
+        @pl.when(ok)
+        def _():
+            move(l, o, who, zs, zi(l, s, way), first).start()
+
+    for l in range(layers):
+        forward(l, 0, 0, q, True)
+        forward(l, 0, 1, q, True)
+        move(l, q, partner, ps, zi(l, 0, 0), True).start()
+    copies = swap_relay(copies, out, sems)
+    for l in range(layers):
+        for s in range(1, line):
+            for way in (0, 1):
+                o = q - s if way == 0 else q + s
+                ok = (o >= 0) if way == 0 else (o < line)
+
+                @pl.when(ok)
+                def _(l=l, s=s, way=way, o=o):
+                    move(l, o, right, zs, zi(l, s - 1, way), False).wait_recv()
+                    move(l, o, partner, ps, zi(l, s, way), False).start()
+                    if s < line - 1:
+                        forward(l, s, way, o, False)
+
+    for l in range(layers):
+        for s in range(line):
+            for way in (0, 1):
+                o = q - s if way == 0 else q + s
+                ok = (o >= 0) if way == 0 else (o < line)
+                if s == 0 and way == 1:
+                    ok = None
+
+                def part(l=l, s=s, way=way, o=o):
+                    copy = move(l, o, partner, ps, zi(l, s, way), False)
+                    copy.wait_send()
+                    remote(
+                        slot(l, o, 1 - core), slot(l, o, 1 - core), ps, zi(l, s, way), partner
+                    ).wait_recv()
+
+                if ok is not None:
+                    pl.when(ok)(part)
+                if s < line - 1:
+                    sent = (
+                        jnp.logical_and(o >= 0, q + 1 < line)
+                        if way == 0
+                        else jnp.logical_and(o < line, q > 0)
+                    )
+
+                    @pl.when(sent)
+                    def _(l=l, s=s, way=way, o=o):
+                        move(l, o, right, zs, zi(l, s, way), False).wait_send()
+
+    swap_end(copies)
+    local.wait()
+    keep.wait()
+
+
+def c_sum(n_dp, g, out, b1, x_out, x_in, keep2, y_out, y_in, keep3, z_out, z_in, a_out, a_in, sems):
+    me, xn, yn, _ = square()
+    line = n_dp // 2
+    dp = lax.axis_index("dp")
+    q, core = dp // 2, dp % 2
+    rows = g.shape[2]
+    rh = rows // 2
+    ry = y_in.shape[1]
+    partner = {"dp": q * 2 + 1 - core}
+    zp = [{"dp": ((q + d) % line) * 2 + core} for d in range(1, line)]
+    mx, my = me % 2, me // 2
+    x_mine = pl.multiple_of(mx * rh, 16)
+    x_give = pl.multiple_of((1 - mx) * rh, 16)
+    y_mine = pl.multiple_of(my * (rh - ry), 16)
+    y_give = pl.multiple_of((1 - my) * (rh - ry), 16)
+    greet([{"space": xn}, {"space": yn}, partner] + zp)
+    give = remote(g.at[:, 1 - core, pl.ds(x_give, rh)], b1.at[:, pl.ds(x_give, rh)], sems, 0, partner)
+    give.start()
+    have = remote(g.at[:, 1 - core, pl.ds(x_mine, rh)], b1.at[:, pl.ds(x_mine, rh)], sems, 1, partner)
+    have.start()
+    give.wait_recv()
+    for l in range(line):
+        x_out[l] = (
+            g[l, core, pl.ds(x_give, rh)].astype(F32) + b1[l, pl.ds(x_give, rh)].astype(F32)
+        ).astype(BF16)
+    sx = remote(x_out, x_in, sems, 2, {"space": xn})
+    sx.start()
+    have.wait_recv()
+    for l in range(line):
+        keep2[l] = g[l, core, pl.ds(x_mine, rh)].astype(F32) + b1[l, pl.ds(x_mine, rh)].astype(F32)
+    sx.wait_recv()
+    for l in range(line):
+        y_out[l] = (
+            keep2[l, pl.ds(y_give, ry)] + x_in[l, pl.ds(y_give, ry)].astype(F32)
+        ).astype(BF16)
+    sy = remote(y_out, y_in, sems, 3, {"space": yn})
+    sy.start()
+    for l in range(line):
+        keep3[l] = keep2[l, pl.ds(y_mine, ry)] + x_in[l, pl.ds(y_mine, ry)].astype(F32)
+    sy.wait_recv()
+    for l in range(line):
+        keep3[l] = keep3[l] + y_in[l].astype(F32)
+    z_out[...] = keep3[...].astype(BF16)
+    moves = []
+    for d in range(1, line):
+        copy = remote(z_out.at[(q + d) % line], z_in.at[d - 1], sems, 3 + d, zp[d - 1])
+        copy.start()
+        moves.append(copy)
+    total = keep3[q]
+    for d, copy in enumerate(moves):
+        copy.wait_recv()
+        total = total + z_in[d].astype(F32)
+    a_out[...] = total.astype(BF16)
+    back = pl.multiple_of(x_mine + y_mine, 16)
+    fy = remote(a_out, a_in.at[0, pl.ds(0, ry)], sems, 3 + line, {"space": yn})
+    fy.start()
+    fx = remote(a_out, a_in.at[1, pl.ds(0, ry)], sems, 4 + line, {"space": xn})
+    fx.start()
+    fy.wait_recv()
+    fz = remote(a_in.at[0, pl.ds(0, ry)], a_in.at[2, pl.ds(0, ry)], sems, 5 + line, {"space": xn})
+    fz.start()
+    out[pl.ds(back, ry)] = a_out[...].astype(F32)
+    out[pl.ds(pl.multiple_of(x_mine + y_give, 16), ry)] = a_in[0].astype(F32)
+    fx.wait_recv()
+    out[pl.ds(pl.multiple_of(x_give + y_mine, 16), ry)] = a_in[1].astype(F32)
+    fz.wait_recv()
+    out[pl.ds(pl.multiple_of(x_give + y_give, 16), ry)] = a_in[2].astype(F32)
+    for copy in [give, have, sx, sy, fy, fx, fz] + moves:
+        copy.wait_send()
+
+
+VM = pl.BlockSpec(memory_space=pltpu.VMEM)
+
+
+def params(cid):
+    return pltpu.CompilerParams(
+        collective_id=cid, has_side_effects=True, vmem_limit_bytes=60 << 20
+    )
+
+
+def swap_strips(strips, cid):
+    dma = pltpu.SemaphoreType.DMA
+    return pl.pallas_call(
+        c_swap,
+        out_shape=jax.ShapeDtypeStruct((4,) + strips.shape, strips.dtype),
+        in_specs=[VM],
+        out_specs=VM,
+        scratch_shapes=[dma((2, 6)), dma],
+        compiler_params=params(cid),
+    )(strips)
+
+
+def open_gather(n_dp, kernels, strips):
+    dma = pltpu.SemaphoreType.DMA
+    shape = kernels.shape
+    whole = shape[:3] + (shape[3] * n_dp, shape[4])
+    return pl.pallas_call(
+        functools.partial(c_open, n_dp),
+        out_shape=(
+            jax.ShapeDtypeStruct(whole, kernels.dtype),
+            jax.ShapeDtypeStruct((4,) + strips.shape, strips.dtype),
+        ),
+        in_specs=[VM, VM],
+        out_specs=(VM, VM),
+        scratch_shapes=[
+            dma((2, 6)),
+            dma((2,)),
+            dma((2, 2 * n_dp)),
+            dma((2, 2 * n_dp)),
+        ],
+        compiler_params=params(0),
+    )(kernels, strips)
+
+
+def sum_grads(n_dp, g, cid):
+    line = n_dp // 2
+    rows, c = g.shape[1:]
+    g = g.reshape(line, 2, rows, c)
+    rh = rows // 2
+    ry = -(-(rh // 2) // 16) * 16
+    vm = pltpu.VMEM
+    return pl.pallas_call(
+        functools.partial(c_sum, n_dp),
+        out_shape=jax.ShapeDtypeStruct((rows, c), F32),
+        in_specs=[VM],
+        out_specs=VM,
+        scratch_shapes=[
+            vm((line, rows, c), BF16),
+            vm((line, rh, c), BF16),
+            vm((line, rh, c), BF16),
+            vm((line, rh, c), F32),
+            vm((line, ry, c), BF16),
+            vm((line, ry, c), BF16),
+            vm((line, ry, c), F32),
+            vm((line, ry, c), BF16),
+            vm((line - 1, ry, c), BF16),
+            vm((ry, c), BF16),
+            vm((3, ry, c), BF16),
+            pltpu.SemaphoreType.DMA((2, 6 + line)),
+        ],
+        compiler_params=params(cid),
+    )(g)
+
+
+def per_device(n_dp, n_sp, inputs, kernels, cotangent, adjacency):
     _, t, s, _, c = inputs.shape
     x0 = inputs[0]
     cot = cotangent[0]
-    weights = [lax.all_gather(kernels[l], "dp", axis=2, tiled=True) for l in range(2)]
+    if n_sp == 4:
+        weights, every = open_gather(n_dp, kernels, edge_strips(x0))
+        rims0 = orient(every.reshape((-1, 4, s, c)), adjacency)
+    else:
+        weights = lax.all_gather(kernels, "dp", axis=3, tiled=True)
+        rims0 = exchange(edge_strips(x0), adjacency, n_sp, 0)
     w1 = weights[0].reshape(3, 3 * c, c)
     w2 = weights[1].reshape(3, 3 * c, c)
     wt = jnp.transpose(weights[1][::-1, ::-1], (0, 1, 3, 2)).reshape(3, 3 * c, c)
@@ -163,7 +488,8 @@
     rim = pl.BlockSpec((1, 4, s, c), lambda i: (i, 0, 0, 0))
     wsp = pl.BlockSpec((3, 3 * c, c), lambda i: (0, 0, 0), pipeline_mode=pl.Buffered(1))
     field = lambda dt: jax.ShapeDtypeStruct((t, s, s, c), dt)
-    dws = jax.ShapeDtypeStruct((3, 3 * c, c), F32)
+    dws = jax.ShapeDtypeStruct((n_dp, 9 * c // n_dp, c), BF16)
+    dwsp = pl.BlockSpec(dws.shape, lambda i: (0, 0, 0))
     x3s = pltpu.VMEM((s + 2, s, 3 * c), BF16)
     accs = pltpu.VMEM((3, c, 3 * c), F32)
     flops = 2 * t * s * s * c * c * 9
@@ -179,11 +505,10 @@
             flops=nf * flops, bytes_accessed=12 << 20, transcendentals=0
         ),
     )
-    rims0 = exchange(edge_strips(x0), adjacency)
     state1, slope1 = call(
-        k_first, 1, [tile, rim, wsp], [tile, tile], [field(BF16), field(BF16)], [x3s]
+        k_first, 1, [tile, rim, wsp], [tile, tile], [field(BF16), field(F32)], [x3s]
     )(x0, rims0, w1)
-    rims1 = exchange(edge_strips(state1), adjacency)
+    rims1 = exchange(edge_strips(state1), adjacency, n_sp, 1)
     state2, g2, rg = call(
         k_last,
         1,
@@ -192,16 +517,14 @@
         [field(BF16), field(BF16), jax.ShapeDtypeStruct((t, 4, s, c), BF16)],
         [x3s, x3s],
     )(state1, rims1, w2, wt, cot)
-    back = exchange(rg, adjacency)
+    back = exchange(rg, adjacency, n_sp, 2)
     up, dw2 = call(
-        k_back, 2, [tile, rim, tile, wsp, tile], [tile, wsp], [field(F32), dws], [x3s, x3s, accs]
+        k_back, 2, [tile, rim, tile, wsp, tile], [tile, dwsp], [field(F32), dws], [x3s, x3s, accs]
     )(state1, rims1, g2, wt, cot)
-    dw2r = reduce_grad(dw2, c)
-    dw1 = call(k_tail, 1, [tile, rim, tile, rim, tile], wsp, dws, [x3s, accs])(
+    dw1 = call(k_tail, 1, [tile, rim, tile, rim, tile], dwsp, dws, [x3s, accs])(
         x0, rims0, up, back, slope1
     )
-    dw1r = reduce_grad(dw1, c)
-    return state2[None], jnp.stack([dw1r, dw2r])
+    return state2[None], reduce_grads(dw1, dw2, n_dp, n_sp)
 
 
 def solution(mesh):
@@ -212,6 +535,7 @@
         P("space", None, None),
     )
     out_specs = (P("dp", "space", None, None, None), P(None, None, None, "dp", None))
+    body = functools.partial(per_device, mesh.shape["dp"], mesh.shape["space"])
     return jax.shard_map(
-        per_device, mesh=mesh, in_specs=in_specs, out_specs=out_specs, check_vma=False
-    )
+        body, mesh=mesh, in_specs=in_specs, out_specs=out_specs, check_vma=False
+    )

time: 311 us -> 199 us (0.64)
  waiting for transfers between devices: 211 us -> 0 us
  Pallas kernels: 62.5 us -> 169 us
  between operations: 14.3 us -> 0.77 us
  local copies, waits for them, and re-layouts: 16.5 us -> 20.2 us
    pallas_call x3 -> x7, Pallas kernels: 46.4 us -> 153 us  [the longest x1 41.3 us: sum_grads(): pl.pallas_call(functools.partial(c_sum, n_dp), out_shape=jax.ShapeDtypeSt...]
    all_gather x5 -> x0, waiting for transfers between devices: 102 us -> none  [the longest x3 71.9 us: exchange(): lax.all_gather(strips, 'space', axis=0, tiled=True)]
    reduce_scatter x2 -> x0, waiting for transfers between devices: 60.3 us -> none  [reduce_grad(): part = lax.psum_scatter(dw, 'dp', scatter_dimension=2, tiled=True)]
    psum x1 -> x0, waiting for transfers between devices: 47.9 us -> none  [reduce_grad(): return lax.psum(part, 'space')]
    pallas_call x0 -> x1, local copies, waits for them, and re-layouts: none -> 3.66 us  [per_device(): call(k_first, 1, [tile, rim, wsp], [tile, tile], [field(BF16), field(F32)...]
  transfers between devices with their start and end apart: 8 -> 0, of which waited for: 8 -> 0; matrix products, arithmetic and copies ran while one was open for 4% -> 0% of each run, Pallas kernels for 15% -> 0%
where the time goes in v2:
time: 199 us; the launch traced here: 198 us
  Pallas kernels  169 us (85%)
  local copies, waits for them, and re-layouts  20.2 us (10%)
  other arithmetic  8.38 us (4%)
    pallas_call x1, Pallas kernels, sum_grads(): pl.pallas_call(functools.partial(c_sum, n_dp), out_shape=jax.ShapeDtypeSt...  41.3 us
    pallas_call x2, Pallas kernels, swap_strips(): pl.pallas_call(c_swap, out_shape=jax.ShapeDtypeStruct((4,) + strips.shape...  36.3 us
    pallas_call x1, Pallas kernels, open_gather(): pl.pallas_call(functools.partial(c_open, n_dp), out_shape=(jax.ShapeDtype...  29.9 us
    pallas_call x1, Pallas kernels, per_device(): call(k_back, 2, [tile, rim, tile, wsp, tile], [tile, dwsp], [field(F32),...  19.9 us
    pallas_call x1, Pallas kernels, per_device(): call(k_last, 1, [tile, rim, wsp, wsp, tile], [tile, tile, rim], [field(BF...  16.2 us
    pallas_call x1, Pallas kernels, per_device(): call(k_tail, 1, [tile, rim, tile, rim, tile], dwsp, dws, [x3s, accs])  13.6 us
    pallas_call x1, Pallas kernels, per_device(): call(k_first, 1, [tile, rim, wsp], [tile, tile], [field(BF16), field(F32)...  11.8 us
    gather x3, local copies, waits for them, and re-layouts, orient(): selected = strips[adjacency[:, :, 0], adjacency[:, :, 1]]  6.36 us

profile of v2, /device:TPU:0, one launch (start us, length us, event | category | flops | bytes accessed | tf_op | source)
XLA Modules:
  0.0 198.2 jit_solution(5399793367507494146)
XLA Ops:
  0.6 0.7 fusion.5
  1.3 0.1 copy.23
  1.4 0.7 fusion.2
  2.1 0.1 copy.26
  2.2 0.1 reshape.35
  2.3 1.0 fusion.7
  3.3 1.7 fusion.8
  5.1 0.8 pad_maximum_fusion.1.src
  5.9 29.9 %shard_map.59 = (bf16[2,3,3,256,256]{4,3,2,1,0:T(8,128)(2,1)}, bf16[4,6,4,32,256]{4,3,2,1,0:T(8,128)(2,1)}) custom-call(bf16[2,3,3,32,256]{4,3,2,1,0:T(8,128)(2,1)} %w_in.1, bf16[6,4,32,256]{3,2,1,0:T(8,128)(2,1)} %pad_maximum_fusion.1.src), custom_call_target="tpu_custom_call" | custom-call | tf_op jit(solution)/shard_map/pallas_call | solution.py:425
  35.7 2.2 %gather_fusion = bf16[24,32,256]{2,1,0:T(8,128)(2,1)S(1)} fusion(bf16[24,4,32,256]{3,2,1,0:T(8,128)(2,1)} %bitcast.52, s32[24]{0:T(128)S(1)} %reshape.35), kind=kCustom, calls=%fused_computation | custom fusion | bytes 786624 | tf_op jit(solution)/shard_map/gather | solution.py:22
  38.0 0.3 rev.12
  38.2 0.9 broadcast_select_fusion.2.rims
  39.1 1.8 slice_bitcast_fusion.2
  41.0 1.5 copy.29
  42.5 11.8 %shard_map.60 = (bf16[6,32,32,256]{3,2,1,0:T(8,128)(2,1)}, f32[6,32,32,256]{3,2,1,0:T(8,128)}) custom-call(bf16[6,32,32,256]{3,2,1,0:T(8,128)(2,1)} %bitcast.50, bf16[6,4,32,256]{3,2,1,0:T(8,128)(2,1)} %broadcast_select_fusion.2.rims, bf16[3,768,256]{2,1,0:T(8,128)(2,1)} %bitcast.47), custom_call_target="tpu_custom_call" | custom-call | flops 7247757312 | bytes 12582912 | tf_op jit(solution)/shard_map/pallas_call | solution.py:508
  54.3 1.0 fusion.6
  55.3 3.7 %copy.27 = bf16[6,32,32,256]{3,1,0,2:T(8,128)(2,1)S(1)} copy(bf16[6,32,32,256]{3,2,1,0:T(8,128)(2,1)} %get-tuple-element.13.x) | data formatting | bytes 6291456 | tf_op jit(solution)/shard_map/pallas_call | solution.py:508
  59.0 0.8 pad_maximum_fusion.2.src
  59.8 19.3 %shard_map.61 = bf16[4,6,4,32,256]{4,3,2,1,0:T(8,128)(2,1)} custom-call(bf16[6,4,32,256]{3,2,1,0:T(8,128)(2,1)} %pad_maximum_fusion.2.src), custom_call_target="tpu_custom_call" | custom-call | tf_op jit(solution)/shard_map/pallas_call | solution.py:411
  79.1 2.1 %gather_fusion.1 = bf16[24,32,256]{2,1,0:T(8,128)(2,1)S(1)} fusion(bf16[24,4,32,256]{3,2,1,0:T(8,128)(2,1)} %bitcast.42, s32[24]{0:T(128)S(1)} %reshape.35), kind=kCustom, calls=%fused_computation.1 | custom fusion | bytes 786624 | tf_op jit(solution)/shard_map/gather | solution.py:22
  81.2 0.3 rev.13
  81.5 0.9 broadcast_select_fusion.1.rims
  82.3 16.2 %shard_map.62 = (bf16[6,32,32,256]{3,2,1,0:T(8,128)(2,1)}, bf16[6,32,32,256]{3,2,1,0:T(8,128)(2,1)}, bf16[6,4,32,256]{3,2,1,0:T(8,128)(2,1)}) custom-call(bf16[6,32,32,256]{3,2,1,0:T(8,128)(2,1)} %get-tuple-element.13.x, bf16[6,4,32,256]{3,2,1,0:T(8,128)(2,1)} %broadcast_select_fusion.1.rims, bf16[3,768,256]{2,1,0:T(8,128)(2,1)} %bitcast.46, ...), custom_call_target="tpu_custom_call" | custom-call | flops 7247757312 | bytes 12582912 | tf_op jit(solution)/shard_map/pallas_call | solution.py:512
  98.5 17.0 %shard_map.64 = bf16[4,6,4,32,256]{4,3,2,1,0:T(8,128)(2,1)} custom-call(bf16[6,4,32,256]{3,2,1,0:T(8,128)(2,1)} %get-tuple-element.17.src), custom_call_target="tpu_custom_call" | custom-call | tf_op jit(solution)/shard_map/pallas_call | solution.py:411
  115.5 2.1 %gather_fusion.2 = bf16[24,32,256]{2,1,0:T(8,128)(2,1)S(1)} fusion(bf16[24,4,32,256]{3,2,1,0:T(8,128)(2,1)} %bitcast.41, s32[24]{0:T(128)S(1)} %reshape.35), kind=kCustom, calls=%fused_computation.2 | custom fusion | bytes 786624 | tf_op jit(solution)/shard_map/gather | solution.py:22
  117.6 0.3 rev.15
  117.9 0.9 broadcast_select_fusion.back
  118.7 19.9 %shard_map.63 = (f32[6,32,32,256]{3,2,1,0:T(8,128)}, bf16[8,288,256]{2,1,0:T(8,128)(2,1)}) custom-call(bf16[6,32,32,256]{3,2,1,0:T(8,128)(2,1)} %get-tuple-element.13.x, bf16[6,4,32,256]{3,2,1,0:T(8,128)(2,1)} %broadcast_select_fusion.1.rims, bf16[6,32,32,256]{3,2,1,0:T(8,128)(2,1)} %get-tuple-element.15.g, bf16[3,768,256]{2,1,0:T(8,128)(2,1)} %bitcast.45, ...), custom_call_target="tpu_custom_call" | custom-call | flops 14495514624 | bytes 12582912 | tf_op jit(solution)/shard_map/pallas_call | solution.py:521
  138.7 13.6 %shard_map.65 = bf16[8,288,256]{2,1,0:T(8,128)(2,1)} custom-call(bf16[6,32,32,256]{3,2,1,0:T(8,128)(2,1)} %bitcast.51, bf16[6,4,32,256]{3,2,1,0:T(8,128)(2,1)} %broadcast_select_fusion.2.rims, f32[6,32,32,256]{3,2,1,0:T(8,128)} %get-tuple-element.16.up, bf16[6,4,32,256]{3,2,1,0:T(8,128)(2,1)} %broadcast_select_fusion.back, ...), custom_call_target="tpu_custom_call" | custom-call | flops 7247757312 | bytes 12582912 | tf_op jit(solution)/shard_map/pallas_call | solution.py:524
  152.2 2.8 %pad_maximum_fusion = bf16[8,576,256]{2,1,0:T(8,128)(2,1)} fusion(bf16[8,288,256]{2,1,0:T(8,128)(2,1)S(1)} %copy-done.1, bf16[8,288,256]{2,1,0:T(8,128)(2,1)} %shard_map.65), kind=kLoop, calls=%fused_computation.3 | loop fusion | flops 4718592 | bytes 4718592 | tf_op jit(solution)/shard_map/concatenate | solution.py:157
  155.1 41.3 %shard_map.66 = f32[576,256]{1,0:T(8,128)} custom-call(bf16[4,2,576,256]{3,2,1,0:T(8,128)(2,1)} %bitcast.34), custom_call_target="tpu_custom_call" | custom-call | tf_op jit(solution)/shard_map/pallas_call | solution.py:450
  196.3 1.9 copy.35
  (7 shorter events, 0.1 us)
Async XLA Ops:
  35.7 3.4 %copy-start = (bf16[2,3,3,256,256]{4,3,2,1,0:T(8,128)(2,1)S(1)}, bf16[2,3,3,256,256]{4,3,2,1,0:T(8,128)(2,1)}, u32[]{:S(2)}) copy-start(bf16[2,3,3,256,256]{4,3,2,1,0:T(8,128)(2,1)} %get-tuple-element.12) | copy-start | bytes 7077892
  138.6 13.6 %copy-start.1 = (bf16[8,288,256]{2,1,0:T(8,128)(2,1)S(1)}, bf16[8,288,256]{2,1,0:T(8,128)(2,1)}, u32[]{:S(2)}) copy-start(bf16[8,288,256]{2,1,0:T(8,128)(2,1)} %get-tuple-element.19) | copy-start | bytes 3538948

commit v3 on v2

--- a/solution.py
+++ b/solution.py
@@ -24,12 +24,8 @@
     return jnp.where(flipped, selected[:, :, ::-1], selected)
 
 
-def exchange(strips, adjacency, n_sp, cid):
-    if n_sp == 4:
-        every = swap_strips(strips, cid).reshape((-1,) + strips.shape[1:])
-    else:
-        every = lax.all_gather(strips, "space", axis=0, tiled=True)
-    return orient(every, adjacency)
+def exchange(strips, adjacency):
+    return orient(lax.all_gather(strips, "space", axis=0, tiled=True), adjacency)
 
 
 def fill(x3, field, rims):
@@ -81,12 +77,37 @@
         )
 
 
+def k_first_send(x, rims, w, adj, state, slope, rims_out, x3, gath, sems):
+    stream_begin()
+    t = rims_out.shape[0]
+    out = k_first(x, rims, w, state, slope, x3)
+    put_strips(gath, t, pl.program_id(0), out)
+    stream_tile(gath, sems, t, adj, rims_out)
+
+
+def k_first_only(*refs):
+    k_first(*refs)
+
+
+def k_last_send(x, rims, w, wt, cot, adj, state, grad, back, x3, g3, rim_grad, gath, sems):
+    stream_begin()
+    t = back.shape[0]
+    k_last(x, rims, w, wt, cot, state, grad, rim_grad, x3, g3)
+    me = lax.axis_index("space")
+    base = (me * t + pl.program_id(0)) * 4
+    for e in range(4):
+        gath[base + e] = rim_grad[0, e]
+    stream_tile(gath, sems, t, adj, back)
+
+
 def k_first(x, rims, w, state, slope, x3):
     fill(x3, x[0], rims[0])
     v = conv(x3, w)
     sg = jax.nn.sigmoid(v)
-    state[0] = (x[0].astype(F32) + v * sg).astype(BF16)
+    out = x[0].astype(F32) + v * sg
+    state[0] = out.astype(BF16)
     slope[0] = (sg * (1.0 + v * (1.0 - sg))).astype(slope.dtype)
+    return out
 
 
 def k_last(x, rims, w, wt, cot, state, grad, rim_grad, x3, g3):
@@ -182,40 +203,91 @@
     return me, xn, yn, (xn + 2) % 4
 
 
-def swap_start(src, out, sems):
+def seg(gath, t, dev, first, count):
+    return gath.at[pl.ds((dev * t + first) * 4, 4 * count)]
+
+
+def send_tiles(gath, sems, t, first, count, i):
     me, xn, yn, _ = square()
-    h = src.shape[0] // 2
-    lo, hi = pl.ds(0, h), pl.ds(h, src.shape[0] - h)
-    copies = [
-        remote(src.at[lo], out.at[me, lo], sems, 0, {"space": xn}),
-        remote(src.at[hi], out.at[me, hi], sems, 1, {"space": yn}),
-        remote(src.at[hi], out.at[me, hi], sems, 2, {"space": xn}),
-        remote(src.at[lo], out.at[me, lo], sems, 3, {"space": yn}),
-    ]
-    for copy in copies:
-        copy.start()
-    return copies
-
-
-def swap_relay(copies, out, sems):
-    me, xn, yn, _ = square()
-    t = out.shape[1]
+    mine = seg(gath, t, me, first, count)
+    remote(mine, mine, sems, i, {"space": xn}).start()
+    remote(mine, mine, sems, t + i, {"space": yn}).start()
+
+
+def relay_tiles(gath, sems, t, first, count, i, by_x):
+    _, xn, yn, _ = square()
+    source, target = (xn, yn) if by_x else (yn, xn)
+    got = seg(gath, t, source, first, count)
+    remote(got, got, sems, i if by_x else t + i, {"space": source}).wait_recv()
+    remote(got, got, sems, 2 * t + i, {"space": target}).start()
+
+
+def drain_tiles(gath, sems, t, first, count, i, by_x):
+    me, xn, yn, dg = square()
+    mine = seg(gath, t, me, first, count)
+    remote(mine, mine, sems, i, {"space": xn}).wait_send()
+    remote(mine, mine, sems, t + i, {"space": yn}).wait_send()
+    source, other = (xn, yn) if by_x else (yn, xn)
+    got = seg(gath, t, source, first, count)
+    remote(got, got, sems, 2 * t + i, {"space": other}).wait_send()
+    late = seg(gath, t, other, first, count)
+    remote(late, late, sems, t + i if by_x else i, {"space": other}).wait_recv()
+    far = seg(gath, t, dg, first, count)
+    remote(far, far, sems, 2 * t + i, {"space": other}).wait_recv()
+
+
+def put_strips(gath, t, i, field):
+    me = lax.axis_index("space")
+    base = (me * t + i) * 4
+    s = field.shape[0]
+    gath[base] = field[0].astype(BF16)
+    gath[base + 1] = field[s - 1].astype(BF16)
+    gath[base + 2] = field[:, 0, :].astype(BF16)
+    gath[base + 3] = field[:, s - 1, :].astype(BF16)
+
+
+def orient_tiles(gath, adj, out):
+    t = out.shape[0]
+    s = out.shape[2]
+    r = lax.broadcasted_iota(jnp.int32, (s, s), 0)
+    c = lax.broadcasted_iota(jnp.int32, (s, s), 1)
+    turn = jnp.where(r + c == s - 1, 1.0, 0.0).astype(BF16)
+
+    def body(a, carry):
+        for e in range(4):
+            line = gath[adj[a, e, 0] * 4 + adj[a, e, 1]]
+            back = jnp.dot(turn, line, preferred_element_type=F32)
+            out[a, e] = jnp.where(adj[a, e, 2] == 1, back, line.astype(F32)).astype(BF16)
+        return carry
+
+    lax.fori_loop(0, t, body, 0)
+
+
+def stream_begin():
+    _, xn, yn, _ = square()
+
+    @pl.when(pl.program_id(0) == 0)
+    def _():
+        greet([{"space": xn}, {"space": yn}])
+
+
+def stream_tile(gath, sems, t, adj, out):
+    i = pl.program_id(0)
     h = t // 2
-    lo, hi = pl.ds(0, h), pl.ds(h, t - h)
-    copies[0].wait_recv()
-    first = remote(out.at[xn, lo], out.at[xn, lo], sems, 4, {"space": yn})
-    first.start()
-    copies[1].wait_recv()
-    second = remote(out.at[yn, hi], out.at[yn, hi], sems, 5, {"space": xn})
-    second.start()
-    return copies + [first, second]
-
-
-def swap_end(copies):
-    for i, copy in enumerate(copies):
-        copy.wait_send()
-        if i >= 2:
-            copy.wait_recv()
+    send_tiles(gath, sems, t, i, 1, i)
+
+    def relay(j):
+        pl.when(j < h)(lambda: relay_tiles(gath, sems, t, j, 1, j, True))
+        pl.when(j >= h)(lambda: relay_tiles(gath, sems, t, j, 1, j, False))
+
+    pl.when(i > 0)(lambda: relay(i - 1))
+
+    @pl.when(i == t - 1)
+    def _():
+        relay(i)
+        for j in range(t):
+            drain_tiles(gath, sems, t, j, 1, j, j < h)
+        orient_tiles(gath, adj, out)
 
 
 def greet(peers):
@@ -227,17 +299,7 @@
     pl.semaphore_wait(barrier, len(peers))
 
 
-def c_swap(src, out, sems, own):
-    me, xn, yn, _ = square()
-    greet([{"space": xn}, {"space": yn}])
-    copies = swap_start(src, out, sems)
-    local = pltpu.make_async_copy(src, out.at[me], own)
-    local.start()
-    swap_end(swap_relay(copies, out, sems))
-    local.wait()
-
-
-def c_open(n_dp, w_in, src, w_out, out, sems, own, zs, ps):
+def c_open(n_dp, w_in, x, adj, w_out, out, gath, sems, own, zs, ps):
     me, xn, yn, _ = square()
     line = n_dp // 2
     dp = lax.axis_index("dp")
@@ -248,15 +310,19 @@
     left = {"dp": ((q + line - 1) % line) * 2 + core}
     partner = {"dp": q * 2 + 1 - core}
     greet([{"space": xn}, {"space": yn}, right, left, partner])
-    copies = swap_start(src, out, sems)
-    local = pltpu.make_async_copy(src, out.at[me], own.at[0])
-    local.start()
+    t = x.shape[0]
+    h = t // 2
+    parts = ((0, h, True), (h, t - h, False))
+
+    def build(a, carry):
+        put_strips(gath, t, a, x[a].astype(F32))
+        return carry
 
     def slot(l, o, c):
         return w_out.at[l, :, :, pl.ds(pl.multiple_of((o * 2 + c) * depth, depth), depth), :]
 
     keep = pltpu.make_async_copy(
-        w_in, w_out.at[:, :, :, pl.ds(pl.multiple_of(dp * depth, depth), depth), :], own.at[1]
+        w_in, w_out.at[:, :, :, pl.ds(pl.multiple_of(dp * depth, depth), depth), :], own
     )
     keep.start()
 
@@ -279,8 +345,13 @@
         forward(l, 0, 0, q, True)
         forward(l, 0, 1, q, True)
         move(l, q, partner, ps, zi(l, 0, 0), True).start()
-    copies = swap_relay(copies, out, sems)
+    lax.fori_loop(0, t, build, 0)
+    for i, (first, count, _) in enumerate(parts):
+        send_tiles(gath, sems, t, first, count, i)
     for l in range(layers):
+        if l == 1:
+            for i, (first, count, by_x) in enumerate(parts):
+                relay_tiles(gath, sems, t, first, count, i, by_x)
         for s in range(1, line):
             for way in (0, 1):
                 o = q - s if way == 0 else q + s
@@ -321,9 +392,10 @@
                     def _(l=l, s=s, way=way, o=o):
                         move(l, o, right, zs, zi(l, s, way), False).wait_send()
 
-    swap_end(copies)
-    local.wait()
+    for i, (first, count, by_x) in enumerate(parts):
+        drain_tiles(gath, sems, t, first, count, i, by_x)
     keep.wait()
+    orient_tiles(gath, adj, out)
 
 
 def c_sum(n_dp, g, out, b1, x_out, x_in, keep2, y_out, y_in, keep3, z_out, z_in, a_out, a_in, sems):
@@ -406,19 +478,7 @@
     )
 
 
-def swap_strips(strips, cid):
-    dma = pltpu.SemaphoreType.DMA
-    return pl.pallas_call(
-        c_swap,
-        out_shape=jax.ShapeDtypeStruct((4,) + strips.shape, strips.dtype),
-        in_specs=[VM],
-        out_specs=VM,
-        scratch_shapes=[dma((2, 6)), dma],
-        compiler_params=params(cid),
-    )(strips)
-
-
-def open_gather(n_dp, kernels, strips):
+def open_gather(n_dp, kernels, x, adjacency):
     dma = pltpu.SemaphoreType.DMA
     shape = kernels.shape
     whole = shape[:3] + (shape[3] * n_dp, shape[4])
@@ -426,18 +486,19 @@
         functools.partial(c_open, n_dp),
         out_shape=(
             jax.ShapeDtypeStruct(whole, kernels.dtype),
-            jax.ShapeDtypeStruct((4,) + strips.shape, strips.dtype),
+            jax.ShapeDtypeStruct((x.shape[0], 4) + x.shape[2:], x.dtype),
         ),
-        in_specs=[VM, VM],
+        in_specs=[VM, VM, pl.BlockSpec(memory_space=pltpu.SMEM)],
         out_specs=(VM, VM),
         scratch_shapes=[
-            dma((2, 6)),
-            dma((2,)),
+            pltpu.VMEM((16 * x.shape[0],) + x.shape[2:], x.dtype),
+            dma((2, 3 * x.shape[0])),
+            dma,
             dma((2, 2 * n_dp)),
             dma((2, 2 * n_dp)),
         ],
         compiler_params=params(0),
-    )(kernels, strips)
+    )(kernels, x, adjacency)
 
 
 def sum_grads(n_dp, g, cid):
@@ -475,11 +536,10 @@
     x0 = inputs[0]
     cot = cotangent[0]
     if n_sp == 4:
-        weights, every = open_gather(n_dp, kernels, edge_strips(x0))
-        rims0 = orient(every.reshape((-1, 4, s, c)), adjacency)
+        weights, rims0 = open_gather(n_dp, kernels, x0, adjacency)
     else:
         weights = lax.all_gather(kernels, "dp", axis=3, tiled=True)
-        rims0 = exchange(edge_strips(x0), adjacency, n_sp, 0)
+        rims0 = exchange(edge_strips(x0), adjacency)
     w1 = weights[0].reshape(3, 3 * c, c)
     w2 = weights[1].reshape(3, 3 * c, c)
     wt = jnp.transpose(weights[1][::-1, ::-1], (0, 1, 3, 2)).reshape(3, 3 * c, c)
@@ -493,31 +553,59 @@
     x3s = pltpu.VMEM((s + 2, s, 3 * c), BF16)
     accs = pltpu.VMEM((3, c, 3 * c), F32)
     flops = 2 * t * s * s * c * c * 9
-    call = lambda body, nf, ins, outs, shapes, scratch: pl.pallas_call(
+    plain = pltpu.CompilerParams(vmem_limit_bytes=60 << 20)
+    call = lambda body, nf, ins, outs, shapes, scratch, extra=plain: pl.pallas_call(
         body,
         grid=(t,),
         in_specs=ins,
         out_specs=outs,
         out_shape=shapes,
         scratch_shapes=scratch,
-        compiler_params=pltpu.CompilerParams(vmem_limit_bytes=60 << 20),
+        compiler_params=extra,
         cost_estimate=pl.CostEstimate(
             flops=nf * flops, bytes_accessed=12 << 20, transcendentals=0
         ),
     )
-    state1, slope1 = call(
-        k_first, 1, [tile, rim, wsp], [tile, tile], [field(BF16), field(F32)], [x3s]
-    )(x0, rims0, w1)
-    rims1 = exchange(edge_strips(state1), adjacency, n_sp, 1)
-    state2, g2, rg = call(
-        k_last,
-        1,
-        [tile, rim, wsp, wsp, tile],
-        [tile, tile, rim],
-        [field(BF16), field(BF16), jax.ShapeDtypeStruct((t, 4, s, c), BF16)],
-        [x3s, x3s],
-    )(state1, rims1, w2, wt, cot)
-    back = exchange(rg, adjacency, n_sp, 2)
+    rims = jax.ShapeDtypeStruct((t, 4, s, c), BF16)
+    if n_sp == 4:
+        smem = pl.BlockSpec(memory_space=pltpu.SMEM)
+        whole = pl.BlockSpec((t, 4, s, c), lambda i: (0, 0, 0, 0))
+        passing = [
+            pltpu.VMEM((16 * t, s, c), BF16),
+            pltpu.SemaphoreType.DMA((2, 3 * t)),
+        ]
+        state1, slope1, rims1 = call(
+            k_first_send,
+            1,
+            [tile, rim, wsp, smem],
+            [tile, tile, whole],
+            [field(BF16), field(F32), rims],
+            [x3s] + passing,
+            params(1),
+        )(x0, rims0, w1, adjacency)
+        state2, g2, back = call(
+            k_last_send,
+            1,
+            [tile, rim, wsp, wsp, tile, smem],
+            [tile, tile, whole],
+            [field(BF16), field(BF16), rims],
+            [x3s, x3s, pltpu.VMEM((1, 4, s, c), BF16)] + passing,
+            params(2),
+        )(state1, rims1, w2, wt, cot, adjacency)
+    else:
+        state1, slope1 = call(
+            k_first_only, 1, [tile, rim, wsp], [tile, tile], [field(BF16), field(F32)], [x3s]
+        )(x0, rims0, w1)
+        rims1 = exchange(edge_strips(state1), adjacency)
+        state2, g2, rg = call(
+            k_last,
+            1,
+            [tile, rim, wsp, wsp, tile],
+            [tile, tile, rim],
+            [field(BF16), field(BF16), rims],
+            [x3s, x3s],
+        )(state1, rims1, w2, wt, cot)
+        back = exchange(rg, adjacency)
     up, dw2 = call(
         k_back, 2, [tile, rim, tile, wsp, tile], [tile, dwsp], [field(F32), dws], [x3s, x3s, accs]
     )(state1, rims1, g2, wt, cot)

time: 199 us -> 175 us (0.88)
  local copies, waits for them, and re-layouts: 20.2 us -> 8.93 us
  Pallas kernels: 169 us -> 161 us
  other arithmetic: 8.38 us -> 3.33 us
    pallas_call x4 -> x2, Pallas kernels: 64.3 us -> 55.1 us  [the longest x1 28.2 us: per_device(): call(k_last_send, 1, [tile, rim, wsp, wsp, tile, smem], [tile, tile, whol...]
    gather x3 -> x0, local copies, waits for them, and re-layouts: 6.36 us -> none  [orient(): selected = strips[adjacency[:, :, 0], adjacency[:, :, 1]]]
    pallas_call x1 -> x0, local copies, waits for them, and re-layouts: 3.66 us -> none  [per_device(): call(k_first, 1, [tile, rim, wsp], [tile, tile], [field(BF16), field(F32)...]
    slice x3 -> x0, local copies, waits for them, and re-layouts: 3.66 us -> none  [the longest x2 1.91 us: edge_strips(): field[:, 0]]
    select_n x3 -> x0, other arithmetic: 2.56 us -> none  [orient(): return jnp.where(flipped, selected[:, :, ::-1], selected)]
where the time goes in v3:
time: 175 us; the launch traced here: 174 us
  Pallas kernels  161 us (92%)
  local copies, waits for them, and re-layouts  8.93 us (5%)
  other arithmetic  3.33 us (2%)
    pallas_call x1, Pallas kernels, sum_grads(): pl.pallas_call(functools.partial(c_sum, n_dp), out_shape=jax.ShapeDtypeSt...  41.2 us
    pallas_call x1, Pallas kernels, open_gather(): pl.pallas_call(functools.partial(c_open, n_dp), out_shape=(jax.ShapeDtype...  31.7 us
    pallas_call x1, Pallas kernels, per_device(): call(k_last_send, 1, [tile, rim, wsp, wsp, tile, smem], [tile, tile, whol...  28.2 us
    pallas_call x1, Pallas kernels, per_device(): call(k_first_send, 1, [tile, rim, wsp, smem], [tile, tile, whole], [field...  26.9 us
    pallas_call x1, Pallas kernels, per_device(): call(k_back, 2, [tile, rim, tile, wsp, tile], [tile, dwsp], [field(F32),...  19.9 us
    pallas_call x1, Pallas kernels, per_device(): call(k_tail, 1, [tile, rim, tile, rim, tile], dwsp, dws, [x3s, accs])  13.4 us
    unnamed x7, local copies, waits for them, and re-layouts  3.88 us

profile of v3, /device:TPU:0, one launch (start us, length us, event | category | flops | bytes accessed | tf_op | source)
XLA Modules:
  0.0 174.4 jit_solution(1338776816640041619)
XLA Ops:
  0.6 1.4 copy.6.adj
  2.0 31.7 %shard_map.59 = (bf16[2,3,3,256,256]{4,3,2,1,0:T(8,128)(2,1)}, bf16[6,4,32,256]{3,2,1,0:T(8,128)(2,1)}) custom-call(bf16[2,3,3,32,256]{4,3,2,1,0:T(8,128)(2,1)} %w_in.1, bf16[6,32,32,256]{3,2,1,0:T(8,128)(2,1)} %bitcast.14, s32[6,4,3]{2,1,0:T(4,128)} %copy.6.adj), custom_call_target="tpu_custom_call" | custom-call | tf_op jit(solution)/shard_map/pallas_call | solution.py:485
  33.8 3.4 %slice_bitcast_fusion = (bf16[3,3,256,256]{3,2,1,0:T(8,128)(2,1)S(1)}, bf16[1,3,3,256,256]{4,3,2,1,0:T(8,128)(2,1)}, bf16[1,3,3,256,256]{4,3,2,1,0:T(8,128)(2,1)}) fusion(bf16[2,3,3,256,256]{4,3,2,1,0:T(8,128)(2,1)} %get-tuple-element.13), kind=kLoop, calls=%fused_computation.2 | loop fusion | bytes 5898240 | tf_op jit(solution)/shard_map/squeeze | solution.py:545
  37.1 0.1 reverse_bitcast_fusion
  37.2 1.6 copy.8
  38.8 26.9 %shard_map.60 = (bf16[6,32,32,256]{3,2,1,0:T(8,128)(2,1)}, f32[6,32,32,256]{3,2,1,0:T(8,128)}, bf16[6,4,32,256]{3,2,1,0:T(8,128)(2,1)}) custom-call(bf16[6,32,32,256]{3,2,1,0:T(8,128)(2,1)} %bitcast.15, bf16[6,4,32,256]{3,2,1,0:T(8,128)(2,1)} %get-tuple-element.12.rims, bf16[3,768,256]{2,1,0:T(8,128)(2,1)} %bitcast.21, s32[6,4,3]{2,1,0:T(4,128)} %copy.6.adj), custom_call_target="tpu_custom_call" | custom-call | flops 7247757312 | bytes 12582912 | tf_op jit(solution)/shard_map/pallas_call | solution.py:577
  65.7 28.2 %shard_map.61 = (bf16[6,32,32,256]{3,2,1,0:T(8,128)(2,1)}, bf16[6,32,32,256]{3,2,1,0:T(8,128)(2,1)}, bf16[6,4,32,256]{3,2,1,0:T(8,128)(2,1)}) custom-call(bf16[6,32,32,256]{3,2,1,0:T(8,128)(2,1)} %get-tuple-element.14.x, bf16[6,4,32,256]{3,2,1,0:T(8,128)(2,1)} %get-tuple-element.15.rims, bf16[3,768,256]{2,1,0:T(8,128)(2,1)} %bitcast.20, ...), custom_call_target="tpu_custom_call" | custom-call | flops 7247757312 | bytes 12582912 | tf_op jit(solution)/shard_map/pallas_call | solution.py:586
  94.0 19.9 %shard_map.62 = (f32[6,32,32,256]{3,2,1,0:T(8,128)}, bf16[8,288,256]{2,1,0:T(8,128)(2,1)}) custom-call(bf16[6,32,32,256]{3,2,1,0:T(8,128)(2,1)} %get-tuple-element.14.x, bf16[6,4,32,256]{3,2,1,0:T(8,128)(2,1)} %get-tuple-element.15.rims, bf16[6,32,32,256]{3,2,1,0:T(8,128)(2,1)} %get-tuple-element.17.g, bf16[3,768,256]{2,1,0:T(8,128)(2,1)} %bitcast.19, ...), custom_call_target="tpu_custom_call" | custom-call | flops 14495514624 | bytes 12582912 | tf_op jit(solution)/shard_map/pallas_call | solution.py:609
  113.9 13.4 %shard_map.63 = bf16[8,288,256]{2,1,0:T(8,128)(2,1)} custom-call(bf16[6,32,32,256]{3,2,1,0:T(8,128)(2,1)} %bitcast.16, bf16[6,4,32,256]{3,2,1,0:T(8,128)(2,1)} %get-tuple-element.12.rims, f32[6,32,32,256]{3,2,1,0:T(8,128)} %get-tuple-element.18.up, bf16[6,4,32,256]{3,2,1,0:T(8,128)(2,1)} %get-tuple-element.19.back, f32[6,32,32,256]{3,2,1,0:T(8,128)} %get-tuple-element.20.slope), custom_call_target="tpu_custom_call" | custom-call | flops 7247757312 | bytes 12582912 | tf_op jit(solution)/shard_map/pallas_call | solution.py:612
  127.3 0.0 copy-start
  127.3 3.3 %pad_maximum_fusion = bf16[8,576,256]{2,1,0:T(8,128)(2,1)} fusion(bf16[8,288,256]{2,1,0:T(8,128)(2,1)} %get-tuple-element.21, bf16[8,288,256]{2,1,0:T(8,128)(2,1)} %shard_map.63), kind=kLoop, calls=%fused_computation | loop fusion | flops 4718592 | bytes 4718592 | tf_op jit(solution)/shard_map/concatenate | solution.py:178
  130.7 41.2 %shard_map.64 = f32[576,256]{1,0:T(8,128)} custom-call(bf16[4,2,576,256]{3,2,1,0:T(8,128)(2,1)} %bitcast.12), custom_call_target="tpu_custom_call" | custom-call | tf_op jit(solution)/shard_map/pallas_call | solution.py:511
  171.9 0.0 copy-done
  171.9 0.0 copy-start.1
  171.9 1.7 copy.12
  173.6 0.0 copy-done.1
  173.6 0.8 copy.13
Async XLA Ops:
  127.3 44.6 %copy-start = (bf16[6,32,32,256]{3,2,1,0:T(8,128)(2,1)S(1)}, bf16[6,32,32,256]{3,2,1,0:T(8,128)(2,1)}, u32[]{:S(2)}) copy-start(bf16[6,32,32,256]{3,2,1,0:T(8,128)(2,1)} %get-tuple-element.16) | copy-start | bytes 9437188
  171.9 1.7 copy-start.1

commit v4 on v3

--- a/solution.py
+++ b/solution.py
@@ -89,15 +89,66 @@
     k_first(*refs)
 
 
-def k_last_send(x, rims, w, wt, cot, adj, state, grad, back, x3, g3, rim_grad, gath, sems):
+def turn_weights(w, wt):
+    c = w.shape[2]
+    for p in range(3):
+        for q in range(3):
+            tap = w[2 - p, (2 - q) * c : (3 - q) * c]
+            wt[p, q * c : (q + 1) * c] = tap.astype(F32).T.astype(BF16)
+
+
+def k_last_send(
+    x, rims, w, cot, adj, state, grad, back, dw, x3, g3, rim_grad, wt, held, acc, gath, sems
+):
+    t = back.shape[0]
+    i = pl.program_id(0)
     stream_begin()
-    t = back.shape[0]
-    k_last(x, rims, w, wt, cot, state, grad, rim_grad, x3, g3)
-    me = lax.axis_index("space")
-    base = (me * t + pl.program_id(0)) * 4
-    for e in range(4):
-        gath[base + e] = rim_grad[0, e]
-    stream_tile(gath, sems, t, adj, back)
+
+    @pl.when(i == 0)
+    def _():
+        turn_weights(w, wt)
+        acc[...] = jnp.zeros_like(acc)
+
+    fill(x3, x[0], rims[0])
+
+    @pl.when(i < t)
+    def _():
+        k_last(x, rims, w, wt, cot, state, grad, rim_grad, x3, g3, False)
+        held[i] = grad[0]
+        me = lax.axis_index("space")
+        base = (me * t + i) * 4
+        for e in range(4):
+            gath[base + e] = rim_grad[0, e]
+
+    stream_tile(gath, sems, t, adj, back, True)
+
+    @pl.when(i >= t)
+    def _():
+        wgrad_add(acc, x3, held[i - t])
+
+    finish_wgrad(acc, dw)
+
+
+def k_tail_send(
+    n_dp, x, rims, g, w, cot, back, slope, dw2, dw, out, x3, g3, wt, acc, *sums
+):
+    i = pl.program_id(0)
+    last = pl.num_programs(0) - 1
+    peers, stages = sum_stages(n_dp, dw2, out, *sums)
+
+    @pl.when(i == 0)
+    def _():
+        greet(peers)
+        stages[0]()
+        turn_weights(w, wt)
+        acc[...] = jnp.zeros_like(acc)
+
+    for k, stage in enumerate(stages[1:-1]):
+        pl.when(i == jnp.minimum(k + 1, last))(stage)
+    fill(g3, g[0], None)
+    tail_tile(x, rims, cot[0].astype(F32) + conv(g3, wt), back, slope, x3, acc)
+    pl.when(i == last)(stages[-1])
+    finish_wgrad(acc, dw)
 
 
 def k_first(x, rims, w, state, slope, x3):
@@ -110,10 +161,11 @@
     return out
 
 
-def k_last(x, rims, w, wt, cot, state, grad, rim_grad, x3, g3):
+def k_last(x, rims, w, wt, cot, state, grad, rim_grad, x3, g3, build=True):
     s = x.shape[1]
     c = x.shape[3]
-    fill(x3, x[0], rims[0])
+    if build:
+        fill(x3, x[0], rims[0])
     v = conv(x3, w)
     sg = jax.nn.sigmoid(v)
     state[0] = (x[0].astype(F32) + v * sg).astype(BF16)
@@ -155,14 +207,9 @@
     finish_wgrad(acc, dw)
 
 
-def k_tail(x, rims, up, back, slope, dw, x3, acc):
-    @pl.when(pl.program_id(0) == 0)
-    def _():
-        acc[...] = jnp.zeros_like(acc)
-
+def tail_tile(x, rims, u, back, slope, x3, acc):
     s = x.shape[1]
     fill(x3, x[0], rims[0])
-    u = up[0]
     row = lax.broadcasted_iota(jnp.int32, u.shape, 0)
     col = lax.broadcasted_iota(jnp.int32, u.shape, 1)
     r = back[0].astype(F32)
@@ -171,18 +218,22 @@
     u = u + jnp.where(col == s - 1, r[3][:, None, :], 0.0)
     g = (u * slope[0].astype(F32)).astype(BF16)
     wgrad_add(acc, x3, g)
+
+
+def k_tail(x, rims, up, back, slope, dw, x3, acc):
+    @pl.when(pl.program_id(0) == 0)
+    def _():
+        acc[...] = jnp.zeros_like(acc)
+
+    tail_tile(x, rims, up[0], back, slope, x3, acc)
     finish_wgrad(acc, dw)
 
 
-def reduce_grads(dw1, dw2, n_dp, n_sp):
+def reduce_grads(dw1, dw2, n_dp):
     both = jnp.concatenate([dw1, dw2], axis=1)
     n, rows, c = both.shape
-    if n_sp == 4:
-        total = sum_grads(n_dp, both, 3)
-    else:
-        part = lax.psum_scatter(both.astype(F32), "dp", scatter_dimension=0, tiled=True)
-        total = lax.psum(part, "space")
-    return total.reshape(LAYERS, 3, 3, c // n, c)
+    part = lax.psum_scatter(both.astype(F32), "dp", scatter_dimension=0, tiled=True)
+    return lax.psum(part, "space").reshape(LAYERS, 3, 3, c // n, c)
 
 
 def remote(src, dst, sems, i, who):
@@ -271,20 +322,27 @@
         greet([{"space": xn}, {"space": yn}])
 
 
-def stream_tile(gath, sems, t, adj, out):
+def stream_tile(gath, sems, t, adj, out, phases=False):
     i = pl.program_id(0)
     h = t // 2
-    send_tiles(gath, sems, t, i, 1, i)
 
     def relay(j):
         pl.when(j < h)(lambda: relay_tiles(gath, sems, t, j, 1, j, True))
         pl.when(j >= h)(lambda: relay_tiles(gath, sems, t, j, 1, j, False))
 
-    pl.when(i > 0)(lambda: relay(i - 1))
-
-    @pl.when(i == t - 1)
-    def _():
-        relay(i)
+    @pl.when(i < t)
+    def _():
+        send_tiles(gath, sems, t, i, 1, i)
+
+    if phases:
+        pl.when(jnp.logical_and(i > 1, i < t + 2))(lambda: relay(i - 2))
+    else:
+        pl.when(i > 0)(lambda: relay(i - 1))
+
+    @pl.when(i == pl.num_programs(0) - 1)
+    def _():
+        if not phases:
+            relay(i)
         for j in range(t):
             drain_tiles(gath, sems, t, j, 1, j, j < h)
         orient_tiles(gath, adj, out)
@@ -398,7 +456,9 @@
     orient_tiles(gath, adj, out)
 
 
-def c_sum(n_dp, g, out, b1, x_out, x_in, keep2, y_out, y_in, keep3, z_out, z_in, a_out, a_in, sems):
+def sum_stages(
+    n_dp, g, out, b1, x_out, x_in, keep2, y_out, y_in, keep3, z_out, z_in, a_out, a_in, sems
+):
     me, xn, yn, _ = square()
     line = n_dp // 2
     dp = lax.axis_index("dp")
@@ -413,60 +473,109 @@
     x_give = pl.multiple_of((1 - mx) * rh, 16)
     y_mine = pl.multiple_of(my * (rh - ry), 16)
     y_give = pl.multiple_of((1 - my) * (rh - ry), 16)
-    greet([{"space": xn}, {"space": yn}, partner] + zp)
-    give = remote(g.at[:, 1 - core, pl.ds(x_give, rh)], b1.at[:, pl.ds(x_give, rh)], sems, 0, partner)
-    give.start()
-    have = remote(g.at[:, 1 - core, pl.ds(x_mine, rh)], b1.at[:, pl.ds(x_mine, rh)], sems, 1, partner)
-    have.start()
-    give.wait_recv()
-    for l in range(line):
-        x_out[l] = (
-            g[l, core, pl.ds(x_give, rh)].astype(F32) + b1[l, pl.ds(x_give, rh)].astype(F32)
-        ).astype(BF16)
-    sx = remote(x_out, x_in, sems, 2, {"space": xn})
-    sx.start()
-    have.wait_recv()
-    for l in range(line):
-        keep2[l] = g[l, core, pl.ds(x_mine, rh)].astype(F32) + b1[l, pl.ds(x_mine, rh)].astype(F32)
-    sx.wait_recv()
-    for l in range(line):
-        y_out[l] = (
-            keep2[l, pl.ds(y_give, ry)] + x_in[l, pl.ds(y_give, ry)].astype(F32)
-        ).astype(BF16)
-    sy = remote(y_out, y_in, sems, 3, {"space": yn})
-    sy.start()
-    for l in range(line):
-        keep3[l] = keep2[l, pl.ds(y_mine, ry)] + x_in[l, pl.ds(y_mine, ry)].astype(F32)
-    sy.wait_recv()
-    for l in range(line):
-        keep3[l] = keep3[l] + y_in[l].astype(F32)
-    z_out[...] = keep3[...].astype(BF16)
-    moves = []
-    for d in range(1, line):
-        copy = remote(z_out.at[(q + d) % line], z_in.at[d - 1], sems, 3 + d, zp[d - 1])
-        copy.start()
-        moves.append(copy)
-    total = keep3[q]
-    for d, copy in enumerate(moves):
-        copy.wait_recv()
-        total = total + z_in[d].astype(F32)
-    a_out[...] = total.astype(BF16)
-    back = pl.multiple_of(x_mine + y_mine, 16)
-    fy = remote(a_out, a_in.at[0, pl.ds(0, ry)], sems, 3 + line, {"space": yn})
-    fy.start()
-    fx = remote(a_out, a_in.at[1, pl.ds(0, ry)], sems, 4 + line, {"space": xn})
-    fx.start()
-    fy.wait_recv()
-    fz = remote(a_in.at[0, pl.ds(0, ry)], a_in.at[2, pl.ds(0, ry)], sems, 5 + line, {"space": xn})
-    fz.start()
-    out[pl.ds(back, ry)] = a_out[...].astype(F32)
-    out[pl.ds(pl.multiple_of(x_mine + y_give, 16), ry)] = a_in[0].astype(F32)
-    fx.wait_recv()
-    out[pl.ds(pl.multiple_of(x_give + y_mine, 16), ry)] = a_in[1].astype(F32)
-    fz.wait_recv()
-    out[pl.ds(pl.multiple_of(x_give + y_give, 16), ry)] = a_in[2].astype(F32)
-    for copy in [give, have, sx, sy, fy, fx, fz] + moves:
-        copy.wait_send()
+    peers = [{"space": xn}, {"space": yn}, partner] + zp
+
+    def half(first, i):
+        return remote(
+            g.at[:, 1 - core, pl.ds(first, rh)], b1.at[:, pl.ds(first, rh)], sems, i, partner
+        )
+
+    give = lambda: half(x_give, 0)
+    have = lambda: half(x_mine, 1)
+    sx = lambda: remote(x_out, x_in, sems, 2, {"space": xn})
+    sy = lambda: remote(y_out, y_in, sems, 3, {"space": yn})
+    sz = lambda d: remote(z_out.at[(q + d) % line], z_in.at[d - 1], sems, 3 + d, zp[d - 1])
+    fy = lambda: remote(a_out, a_in.at[0], sems, 3 + line, {"space": yn})
+    fx = lambda: remote(a_out, a_in.at[1], sems, 4 + line, {"space": xn})
+    fz = lambda: remote(a_in.at[0], a_in.at[2], sems, 5 + line, {"space": xn})
+
+    def s0():
+        give().start()
+        have().start()
+
+    def s1():
+        give().wait_recv()
+        for l in range(line):
+            x_out[l] = (
+                g[l, core, pl.ds(x_give, rh)].astype(F32) + b1[l, pl.ds(x_give, rh)].astype(F32)
+            ).astype(BF16)
+        sx().start()
+        have().wait_recv()
+        for l in range(line):
+            keep2[l] = g[l, core, pl.ds(x_mine, rh)].astype(F32) + b1[
+                l, pl.ds(x_mine, rh)
+            ].astype(F32)
+
+    def s2():
+        sx().wait_recv()
+        for l in range(line):
+            y_out[l] = (
+                keep2[l, pl.ds(y_give, ry)] + x_in[l, pl.ds(y_give, ry)].astype(F32)
+            ).astype(BF16)
+        sy().start()
+        for l in range(line):
+            keep3[l] = keep2[l, pl.ds(y_mine, ry)] + x_in[l, pl.ds(y_mine, ry)].astype(F32)
+
+    def s3():
+        sy().wait_recv()
+        for l in range(line):
+            keep3[l] = keep3[l] + y_in[l].astype(F32)
+        z_out[...] = keep3[...].astype(BF16)
+        for d in range(1, line):
+            sz(d).start()
+
+    def s4():
+        total = keep3[q]
+        for d in range(1, line):
+            sz(d).wait_recv()
+            total = total + z_in[d - 1].astype(F32)
+        a_out[...] = total.astype(BF16)
+        fy().start()
+        fx().start()
+
+    def s5():
+        fy().wait_recv()
+        fz().start()
+        out[pl.ds(pl.multiple_of(x_mine + y_mine, 16), ry)] = a_out[...].astype(F32)
+        out[pl.ds(pl.multiple_of(x_mine + y_give, 16), ry)] = a_in[0].astype(F32)
+        fx().wait_recv()
+        out[pl.ds(pl.multiple_of(x_give + y_mine, 16), ry)] = a_in[1].astype(F32)
+        fz().wait_recv()
+        out[pl.ds(pl.multiple_of(x_give + y_give, 16), ry)] = a_in[2].astype(F32)
+        for copy in [give, have, sx, sy, fy, fx, fz]:
+            copy().wait_send()
+        for d in range(1, line):
+            sz(d).wait_send()
+
+    return peers, [s0, s1, s2, s3, s4, s5]
+
+
+def c_sum(n_dp, *refs):
+    peers, stages = sum_stages(n_dp, *refs)
+    greet(peers)
+    for stage in stages:
+        stage()
+
+
+def sum_scratch(n_dp, rows, c):
+    line = n_dp // 2
+    rh = rows // 2
+    ry = -(-(rh // 2) // 16) * 16
+    vm = pltpu.VMEM
+    return [
+        vm((line, rows, c), BF16),
+        vm((line, rh, c), BF16),
+        vm((line, rh, c), BF16),
+        vm((line, rh, c), F32),
+        vm((line, ry, c), BF16),
+        vm((line, ry, c), BF16),
+        vm((line, ry, c), F32),
+        vm((line, ry, c), BF16),
+        vm((line - 1, ry, c), BF16),
+        vm((ry, c), BF16),
+        vm((3, ry, c), BF16),
+        pltpu.SemaphoreType.DMA((2, 6 + line)),
+    ]
 
 
 VM = pl.BlockSpec(memory_space=pltpu.VMEM)
@@ -504,31 +613,14 @@
 def sum_grads(n_dp, g, cid):
     line = n_dp // 2
     rows, c = g.shape[1:]
-    g = g.reshape(line, 2, rows, c)
-    rh = rows // 2
-    ry = -(-(rh // 2) // 16) * 16
-    vm = pltpu.VMEM
     return pl.pallas_call(
         functools.partial(c_sum, n_dp),
         out_shape=jax.ShapeDtypeStruct((rows, c), F32),
         in_specs=[VM],
         out_specs=VM,
-        scratch_shapes=[
-            vm((line, rows, c), BF16),
-            vm((line, rh, c), BF16),
-            vm((line, rh, c), BF16),
-            vm((line, rh, c), F32),
-            vm((line, ry, c), BF16),
-            vm((line, ry, c), BF16),
-            vm((line, ry, c), F32),
-            vm((line, ry, c), BF16),
-            vm((line - 1, ry, c), BF16),
-            vm((ry, c), BF16),
-            vm((3, ry, c), BF16),
-            pltpu.SemaphoreType.DMA((2, 6 + line)),
-        ],
+        scratch_shapes=sum_scratch(n_dp, rows, c),
         compiler_params=params(cid),
-    )(g)
+    )(g.reshape(line, 2, rows, c))
 
 
 def per_device(n_dp, n_sp, inputs, kernels, cotangent, adjacency):
@@ -554,9 +646,9 @@
     accs = pltpu.VMEM((3, c, 3 * c), F32)
     flops = 2 * t * s * s * c * c * 9
     plain = pltpu.CompilerParams(vmem_limit_bytes=60 << 20)
-    call = lambda body, nf, ins, outs, shapes, scratch, extra=plain: pl.pallas_call(
+    call = lambda body, nf, ins, outs, shapes, scratch, extra=plain, steps=t: pl.pallas_call(
         body,
-        grid=(t,),
+        grid=(steps,),
         in_specs=ins,
         out_specs=outs,
         out_shape=shapes,
@@ -583,15 +675,37 @@
             [x3s] + passing,
             params(1),
         )(x0, rims0, w1, adjacency)
-        state2, g2, back = call(
+        twice = pl.BlockSpec((1, s, s, c), lambda i: (i % t, 0, 0, 0))
+        rim2 = pl.BlockSpec((1, 4, s, c), lambda i: (i % t, 0, 0, 0))
+        once = pl.BlockSpec((1, s, s, c), lambda i: (jnp.minimum(i, t - 1), 0, 0, 0))
+        wts = pltpu.VMEM((3, 3 * c, c), BF16)
+        state2, g2, back, dw2 = call(
             k_last_send,
-            1,
-            [tile, rim, wsp, wsp, tile, smem],
-            [tile, tile, whole],
-            [field(BF16), field(BF16), rims],
-            [x3s, x3s, pltpu.VMEM((1, 4, s, c), BF16)] + passing,
+            2,
+            [twice, rim2, wsp, once, smem],
+            [once, once, whole, dwsp],
+            [field(BF16), field(BF16), rims, dws],
+            [x3s, x3s, pltpu.VMEM((1, 4, s, c), BF16), wts, pltpu.VMEM((t, s, s, c), BF16), accs]
+            + passing,
             params(2),
-        )(state1, rims1, w2, wt, cot, adjacency)
+            2 * t,
+        )(state1, rims1, w2, cot, adjacency)
+        rows = dws.shape[1]
+        line = n_dp // 2
+        wide = pl.BlockSpec((line, 2, rows, c), lambda i: (0, 0, 0, 0))
+        flat = pl.BlockSpec((rows, c), lambda i: (0, 0))
+        total = jax.ShapeDtypeStruct((rows, c), F32)
+        dw1, sum2 = call(
+            functools.partial(k_tail_send, n_dp),
+            2,
+            [tile, rim, tile, wsp, tile, rim, tile, wide],
+            [dwsp, flat],
+            [dws, total],
+            [x3s, x3s, wts, accs] + sum_scratch(n_dp, rows, c),
+            params(4),
+        )(x0, rims0, g2, w2, cot, back, slope1, dw2.reshape(line, 2, rows, c))
+        sum1 = sum_grads(n_dp, dw1, 3)
+        grads = jnp.stack([sum1, sum2]).reshape(LAYERS, 3, 3, c // n_dp, c)
     else:
         state1, slope1 = call(
             k_first_only, 1, [tile, rim, wsp], [tile, tile], [field(BF16), field(F32)], [x3s]
@@ -606,13 +720,19 @@
             [x3s, x3s],
         )(state1, rims1, w2, wt, cot)
         back = exchange(rg, adjacency)
-    up, dw2 = call(
-        k_back, 2, [tile, rim, tile, wsp, tile], [tile, dwsp], [field(F32), dws], [x3s, x3s, accs]
-    )(state1, rims1, g2, wt, cot)
-    dw1 = call(k_tail, 1, [tile, rim, tile, rim, tile], dwsp, dws, [x3s, accs])(
-        x0, rims0, up, back, slope1
-    )
-    return state2[None], reduce_grads(dw1, dw2, n_dp, n_sp)
+        up, dw2 = call(
+            k_back,
+            2,
+            [tile, rim, tile, wsp, tile],
+            [tile, dwsp],
+            [field(F32), dws],
+            [x3s, x3s, accs],
+        )(state1, rims1, g2, wt, cot)
+        dw1 = call(k_tail, 1, [tile, rim, tile, rim, tile], dwsp, dws, [x3s, accs])(
+            x0, rims0, up, back, slope1
+        )
+        grads = reduce_grads(dw1, dw2, n_dp)
+    return state2[None], grads
 
 
 def solution(mesh):

time: 175 us -> 175 us (level)
  Pallas kernels: 161 us -> 165 us
  local copies, waits for them, and re-layouts: 8.93 us -> 6.32 us
    pallas_call x3 -> x2, Pallas kernels: 61.6 us -> 77.6 us  [the longest x1 42.8 us: per_device(): call(functools.partial(k_tail_send, n_dp), 2, [tile, rim, tile, wsp, tile...]
    pallas_call x1, Pallas kernels: 41.2 us -> 29.1 us  [sum_grads(): pl.pallas_call(functools.partial(c_sum, n_dp), out_shape=jax.ShapeDtypeSt...]
    squeeze x1 -> x0, local copies, waits for them, and re-layouts: 3.36 us -> none  [per_device(): weights[1][::-1, ::-1]]
    concatenate x1 -> x0, other arithmetic: 3.33 us -> none  [reduce_grads(): both = jnp.concatenate([dw1, dw2], axis=1)]
    slice x0 -> x1, local copies, waits for them, and re-layouts: none -> 3.26 us  [per_device(): w2 = weights[1].reshape(3, 3 * c, c)]
    another operation x0 -> x1, other arithmetic: none -> 1.92 us  [per_device(): grads = jnp.stack([sum1, sum2]).reshape(LAYERS, 3, 3, c // n_dp, c)]
    unnamed x7 -> x4, local copies, waits for them, and re-layouts: 3.88 us -> 3.06 us
where the time goes in v4:
time: 175 us; the launch traced here: 174 us
  Pallas kernels  165 us (94%)
  local copies, waits for them, and re-layouts  6.32 us (4%)
  other arithmetic  1.92 us (1%)
    pallas_call x1, Pallas kernels, per_device(): call(functools.partial(k_tail_send, n_dp), 2, [tile, rim, tile, wsp, tile...  42.8 us
    pallas_call x1, Pallas kernels, per_device(): call(k_last_send, 2, [twice, rim2, wsp, once, smem], [once, once, whole,...  34.8 us
    pallas_call x1, Pallas kernels, open_gather(): pl.pallas_call(functools.partial(c_open, n_dp), out_shape=(jax.ShapeDtype...  31.7 us
    pallas_call x1, Pallas kernels, sum_grads(): pl.pallas_call(functools.partial(c_sum, n_dp), out_shape=jax.ShapeDtypeSt...  29.1 us
    pallas_call x1, Pallas kernels, per_device(): call(k_first_send, 1, [tile, rim, wsp, smem], [tile, tile, whole], [field...  27 us

profile of v4, /device:TPU:0, one launch (start us, length us, event | category | flops | bytes accessed | tf_op | source)
XLA Modules:
  0.0 174.3 jit_solution(10318120753868388543)
XLA Ops:
  0.6 1.4 copy.6.adj
  2.0 31.7 %shard_map.59 = (bf16[2,3,3,256,256]{4,3,2,1,0:T(8,128)(2,1)}, bf16[6,4,32,256]{3,2,1,0:T(8,128)(2,1)}) custom-call(bf16[2,3,3,32,256]{4,3,2,1,0:T(8,128)(2,1)} %w_in.1, bf16[6,32,32,256]{3,2,1,0:T(8,128)(2,1)} %bitcast.10, s32[6,4,3]{2,1,0:T(4,128)} %copy.6.adj), custom_call_target="tpu_custom_call" | custom-call | tf_op jit(solution)/shard_map/pallas_call | solution.py:594
  33.8 3.3 %fusion = (bf16[1,3,3,256,256]{4,3,2,1,0:T(8,128)(2,1)}, bf16[1,3,3,256,256]{4,3,2,1,0:T(8,128)(2,1)}) fusion(bf16[2,3,3,256,256]{4,3,2,1,0:T(8,128)(2,1)} %get-tuple-element.14), kind=kLoop, calls=%fused_computation.1 | loop fusion | bytes 4718592 | tf_op jit(solution)/shard_map/slice | solution.py:636
  37.0 27.0 %shard_map.60 = (bf16[6,32,32,256]{3,2,1,0:T(8,128)(2,1)}, f32[6,32,32,256]{3,2,1,0:T(8,128)}, bf16[6,4,32,256]{3,2,1,0:T(8,128)(2,1)}) custom-call(bf16[6,32,32,256]{3,2,1,0:T(8,128)(2,1)} %bitcast.11, bf16[6,4,32,256]{3,2,1,0:T(8,128)(2,1)} %get-tuple-element.13.rims, bf16[3,768,256]{2,1,0:T(8,128)(2,1)} %bitcast.16, s32[6,4,3]{2,1,0:T(4,128)} %copy.6.adj), custom_call_target="tpu_custom_call" | custom-call | flops 7247757312 | bytes 12582912 | tf_op jit(solution)/shard_map/pallas_call | solution.py:669
  64.0 34.8 %shard_map.61 = (bf16[6,32,32,256]{3,2,1,0:T(8,128)(2,1)}, bf16[6,32,32,256]{3,2,1,0:T(8,128)(2,1)}, bf16[6,4,32,256]{3,2,1,0:T(8,128)(2,1)}, bf16[8,288,256]{2,1,0:T(8,128)(2,1)}) custom-call(bf16[6,32,32,256]{3,2,1,0:T(8,128)(2,1)} %get-tuple-element.15.x, bf16[6,4,32,256]{3,2,1,0:T(8,128)(2,1)} %get-tuple-element.16.rims, bf16[3,768,256]{2,1,0:T(8,128)(2,1)} %bitcast.14, ...), custom_call_target="tpu_custom_call" | custom-call | flops 14495514624 | bytes 12582912 | tf_op jit(solution)/shard_map/pallas_call | solution.py:682
  98.8 0.0 copy-start
  98.8 42.8 %shard_map.62 = (bf16[8,288,256]{2,1,0:T(8,128)(2,1)}, f32[288,256]{1,0:T(8,128)}) custom-call(bf16[6,32,32,256]{3,2,1,0:T(8,128)(2,1)} %bitcast.12, bf16[6,4,32,256]{3,2,1,0:T(8,128)(2,1)} %get-tuple-element.13.rims, bf16[6,32,32,256]{3,2,1,0:T(8,128)(2,1)} %get-tuple-element.18.g, bf16[3,768,256]{2,1,0:T(8,128)(2,1)} %bitcast.15, ...), custom_call_target="tpu_custom_call" | custom-call | flops 14495514624 | bytes 12582912 | tf_op jit(solution)/shard_map/pallas_call | solution.py:698
  141.6 29.1 %shard_map.63 = f32[288,256]{1,0:T(8,128)} custom-call(bf16[4,2,288,256]{3,2,1,0:T(8,128)(2,1)} %bitcast.13), custom_call_target="tpu_custom_call" | custom-call | tf_op jit(solution)/shard_map/pallas_call | solution.py:616
  170.7 1.9 %pad_maximum_fusion = f32[2,3,3,32,256]{4,3,2,1,0:T(8,128)} fusion(f32[1,3,3,32,256]{4,3,2,1,0:T(8,128)} %bitcast.18, f32[1,3,3,32,256]{4,3,2,1,0:T(8,128)} %bitcast.17), kind=kLoop, calls=%fused_computation | loop fusion | flops 147456 | bytes 1179648 | tf_op jit(solution)/shard_map/stack | solution.py:708
  172.7 0.0 copy-done
  172.7 1.7 copy.10
Async XLA Ops:
  98.8 73.8 %copy-start = (bf16[6,32,32,256]{3,2,1,0:T(8,128)(2,1)S(1)}, bf16[6,32,32,256]{3,2,1,0:T(8,128)(2,1)}, u32[]{:S(2)}) copy-start(bf16[6,32,32,256]{3,2,1,0:T(8,128)(2,1)} %get-tuple-element.17) | copy-start | bytes 9437188

commit v5 on v4

--- a/solution.py
+++ b/solution.py
@@ -143,12 +143,16 @@
         turn_weights(w, wt)
         acc[...] = jnp.zeros_like(acc)
 
-    for k, stage in enumerate(stages[1:-1]):
-        pl.when(i == jnp.minimum(k + 1, last))(stage)
+    for step, stage in ((2, stages[1]), (4, stages[2]), (5, stages[3])):
+        pl.when(i == jnp.minimum(step, last))(stage)
     fill(g3, g[0], None)
     tail_tile(x, rims, cot[0].astype(F32) + conv(g3, wt), back, slope, x3, acc)
-    pl.when(i == last)(stages[-1])
     finish_wgrad(acc, dw)
+
+    @pl.when(i == last)
+    def _():
+        stages[4]()
+        stages[5]()
 
 
 def k_first(x, rims, w, state, slope, x3):

time: 175 us -> 176 us (level)
  no operation moved by 1% of the time
where the time goes in v5:
time: 176 us; the launch traced here: 175 us
  Pallas kernels  166 us (94%)
  local copies, waits for them, and re-layouts  6.32 us (4%)
  other arithmetic  1.92 us (1%)
    pallas_call x1, Pallas kernels, per_device(): call(functools.partial(k_tail_send, n_dp), 2, [tile, rim, tile, wsp, tile...  43.7 us
    pallas_call x1, Pallas kernels, per_device(): call(k_last_send, 2, [twice, rim2, wsp, once, smem], [once, once, whole,...  34.8 us
    pallas_call x1, Pallas kernels, open_gather(): pl.pallas_call(functools.partial(c_open, n_dp), out_shape=(jax.ShapeDtype...  31.7 us
    pallas_call x1, Pallas kernels, sum_grads(): pl.pallas_call(functools.partial(c_sum, n_dp), out_shape=jax.ShapeDtypeSt...  29.1 us
    pallas_call x1, Pallas kernels, per_device(): call(k_first_send, 1, [tile, rim, wsp, smem], [tile, tile, whole], [field...  27 us

profile of v5, /device:TPU:0, one launch (start us, length us, event | category | flops | bytes accessed | tf_op | source)
XLA Modules:
  0.0 175.2 jit_solution(9840993569214764940)
XLA Ops:
  0.6 1.4 copy.6.adj
  2.0 31.7 %shard_map.59 = (bf16[2,3,3,256,256]{4,3,2,1,0:T(8,128)(2,1)}, bf16[6,4,32,256]{3,2,1,0:T(8,128)(2,1)}) custom-call(bf16[2,3,3,32,256]{4,3,2,1,0:T(8,128)(2,1)} %w_in.1, bf16[6,32,32,256]{3,2,1,0:T(8,128)(2,1)} %bitcast.10, s32[6,4,3]{2,1,0:T(4,128)} %copy.6.adj), custom_call_target="tpu_custom_call" | custom-call | tf_op jit(solution)/shard_map/pallas_call | solution.py:598
  33.8 3.3 %fusion = (bf16[1,3,3,256,256]{4,3,2,1,0:T(8,128)(2,1)}, bf16[1,3,3,256,256]{4,3,2,1,0:T(8,128)(2,1)}) fusion(bf16[2,3,3,256,256]{4,3,2,1,0:T(8,128)(2,1)} %get-tuple-element.14), kind=kLoop, calls=%fused_computation.1 | loop fusion | bytes 4718592 | tf_op jit(solution)/shard_map/slice | solution.py:640
  37.0 27.0 %shard_map.60 = (bf16[6,32,32,256]{3,2,1,0:T(8,128)(2,1)}, f32[6,32,32,256]{3,2,1,0:T(8,128)}, bf16[6,4,32,256]{3,2,1,0:T(8,128)(2,1)}) custom-call(bf16[6,32,32,256]{3,2,1,0:T(8,128)(2,1)} %bitcast.11, bf16[6,4,32,256]{3,2,1,0:T(8,128)(2,1)} %get-tuple-element.13.rims, bf16[3,768,256]{2,1,0:T(8,128)(2,1)} %bitcast.16, s32[6,4,3]{2,1,0:T(4,128)} %copy.6.adj), custom_call_target="tpu_custom_call" | custom-call | flops 7247757312 | bytes 12582912 | tf_op jit(solution)/shard_map/pallas_call | solution.py:673
  64.0 34.8 %shard_map.61 = (bf16[6,32,32,256]{3,2,1,0:T(8,128)(2,1)}, bf16[6,32,32,256]{3,2,1,0:T(8,128)(2,1)}, bf16[6,4,32,256]{3,2,1,0:T(8,128)(2,1)}, bf16[8,288,256]{2,1,0:T(8,128)(2,1)}) custom-call(bf16[6,32,32,256]{3,2,1,0:T(8,128)(2,1)} %get-tuple-element.15.x, bf16[6,4,32,256]{3,2,1,0:T(8,128)(2,1)} %get-tuple-element.16.rims, bf16[3,768,256]{2,1,0:T(8,128)(2,1)} %bitcast.14, ...), custom_call_target="tpu_custom_call" | custom-call | flops 14495514624 | bytes 12582912 | tf_op jit(solution)/shard_map/pallas_call | solution.py:686
  98.8 0.0 copy-start
  98.8 43.7 %shard_map.62 = (bf16[8,288,256]{2,1,0:T(8,128)(2,1)}, f32[288,256]{1,0:T(8,128)}) custom-call(bf16[6,32,32,256]{3,2,1,0:T(8,128)(2,1)} %bitcast.12, bf16[6,4,32,256]{3,2,1,0:T(8,128)(2,1)} %get-tuple-element.13.rims, bf16[6,32,32,256]{3,2,1,0:T(8,128)(2,1)} %get-tuple-element.18.g, bf16[3,768,256]{2,1,0:T(8,128)(2,1)} %bitcast.15, ...), custom_call_target="tpu_custom_call" | custom-call | flops 14495514624 | bytes 12582912 | tf_op jit(solution)/shard_map/pallas_call | solution.py:702
  142.5 29.1 %shard_map.63 = f32[288,256]{1,0:T(8,128)} custom-call(bf16[4,2,288,256]{3,2,1,0:T(8,128)(2,1)} %bitcast.13), custom_call_target="tpu_custom_call" | custom-call | tf_op jit(solution)/shard_map/pallas_call | solution.py:620
  171.6 1.9 %pad_maximum_fusion = f32[2,3,3,32,256]{4,3,2,1,0:T(8,128)} fusion(f32[1,3,3,32,256]{4,3,2,1,0:T(8,128)} %bitcast.18, f32[1,3,3,32,256]{4,3,2,1,0:T(8,128)} %bitcast.17), kind=kLoop, calls=%fused_computation | loop fusion | flops 147456 | bytes 1179648 | tf_op jit(solution)/shard_map/stack | solution.py:712
  173.6 0.0 copy-done
  173.6 1.7 copy.10
Async XLA Ops:
  98.8 74.7 %copy-start = (bf16[6,32,32,256]{3,2,1,0:T(8,128)(2,1)S(1)}, bf16[6,32,32,256]{3,2,1,0:T(8,128)(2,1)}, u32[]{:S(2)}) copy-start(bf16[6,32,32,256]{3,2,1,0:T(8,128)(2,1)} %get-tuple-element.17) | copy-start | bytes 9437188
